TPU v7x, 32 devices: a whole 2x2x4 slice. The times are simulated.
32 devices in a mesh: val: 4 (over x, core), cond: 8 (over z, y).
Axes of the slice: x: 2, y: 2, z: 4, core: 2. Of those that a mesh axis runs over, the one named last changes fastest.
Arguments:
- val_orbitals: bfloat16 [16, 768], P('val'), may hold values from -6 to 6
- cond_orbitals: bfloat16 [64, 768], P('cond'), may hold values from -6 to 6
- val_energy: bfloat16 [16], P('val'), may hold values from -0.59765625 to -0.049804688
- cond_energy: bfloat16 [64], P('cond'), may hold values from 0.049804688 to 1.1953125
- wave_index: int32 [4096], P('cond'), may hold values from 0 to 884735
Outputs:
- chi_real: float32 [128, 4096], P('val', 'cond')
- chi_imag: float32 [128, 4096], P('val', 'cond')
Inputs may be any that keep to these rules, and one draw needn't show every extreme that they name: `wave_index`: values may repeat.
All inputs are finite; a program needn't handle non-finite values.
Results may differ from a plain program's by a relative error of at most 0.0037.
Values may be sent and summed in bfloat16 or wider, within the bound.
A program may use at most 64 MiB of HBM per device.

v0:
```python
import functools
import math

import jax
import jax.numpy as jnp
from jax import lax
from jax.experimental import pallas as pl
from jax.experimental.pallas import tpu as pltpu
from jax.sharding import PartitionSpec as P

NG = 96
NW = 128
SLAB_Y = 4
LANES = 128
VMEM_LIMIT = 24 * 1024 * 1024
MESH = pl.DeviceIdType.MESH


def modulo(value, period):
    return value - period * jnp.floor((value + 0.5) * (1.0 / period))


def cos_turns(turns):
    angle = (turns - NG / 2) * (math.pi / NG)
    square = angle * angle
    series = 1.0
    for order in (10, 8, 6, 4, 2):
        series = 1.0 - square * series * (1.0 / (order * (order + 1)))
    sine = angle * series
    return 2.0 * sine * sine - 1.0


def wave_parts(index):
    flat = index.astype(jnp.float32)
    wave_x = jnp.floor((flat + 0.5) * (1.0 / (NG * NG)))
    rest = flat - wave_x * (NG * NG)
    wave_y = jnp.floor((rest + 0.5) * (1.0 / NG))
    return wave_x, wave_y, rest - wave_y * NG


def factors(index, points, shift):
    wave_x, wave_y, wave_z = wave_parts(index)
    planes = points // NG
    along_x = lax.broadcasted_iota(jnp.int32, (NG, LANES), 0).astype(jnp.float32)
    plane = lax.broadcasted_iota(jnp.int32, (planes, LANES), 0).astype(jnp.float32)
    along_z = jnp.floor((plane + 0.5) * (1.0 / SLAB_Y))
    along_y = plane - along_z * SLAB_Y
    turns_x = modulo(along_x * wave_x, NG)
    turns_yz = modulo(along_y * wave_y + along_z * wave_z + shift, NG)
    quarter = 3 * NG // 4
    return (
        cos_turns(turns_x),
        cos_turns(modulo(turns_x + quarter, NG)),
        cos_turns(turns_yz),
        cos_turns(modulo(turns_yz + quarter, NG)),
    )


def split(value):
    high = value.astype(jnp.bfloat16)
    low = (value - high.astype(jnp.float32)).astype(jnp.bfloat16)
    return jnp.concatenate([high, low], axis=0)


def dot(left, right):
    return jnp.dot(left, right, preferred_element_type=jnp.float32)


def partner(position, offset, size):
    if size & (size - 1):
        return lax.rem(position + offset, size)
    bit = 1
    while bit < size:
        if offset & bit:
            position = position + bit - 2 * bit * lax.rem(position // bit, 2)
        bit *= 2
    return position


def source(position, offset, size):
    if size & (size - 1):
        return lax.rem(position + size - offset, size)
    return partner(position, offset, size)


def kernel(
    nv, nc, group, slots,
    val, cond, val_energy, cond_energy, wave, out,
    gath_v, gath_c, gath_ve, gath_ce, own_wave, window, cos_rows, sin_rows, window_table, dens, totals,
    send_v, recv_v, send_c, recv_c, send_ve, recv_ve, send_ce, recv_ce, send_w, recv_w, local,
):
    iv = lax.axis_index("val")
    ic = lax.axis_index("cond")
    vb, points = val.shape
    cb = cond.shape[0]
    rows = NW // nv
    planes = points // NG

    barrier = pltpu.get_barrier_semaphore()
    for d in range(nc - 1, 0, -1):
        pl.semaphore_signal(barrier, inc=1, device_id={"cond": partner(ic, d, nc)}, device_id_type=MESH)
    for d in range(1, nv):
        pl.semaphore_signal(barrier, inc=1, device_id={"val": partner(iv, d, nv)}, device_id_type=MESH)

    wave_copy = pltpu.make_async_copy(wave, own_wave, local.at[0])
    own_copies = [
        pltpu.make_async_copy(val, gath_v.at[iv], local.at[1]),
        pltpu.make_async_copy(val_energy, gath_ve.at[iv], local.at[2]),
        pltpu.make_async_copy(cond, gath_c.at[ic], local.at[3]),
        pltpu.make_async_copy(cond_energy, gath_ce.at[ic], local.at[4]),
    ]
    wave_copy.start()
    for copy in own_copies:
        copy.start()
    wave_copy.wait()
    for copy in own_copies:
        copy.wait()
    pl.semaphore_wait(barrier, nc - 1 + nv - 1)

    def window_copy(d):
        return pltpu.make_async_remote_copy(
            src_ref=own_wave.at[pl.ds(0, 1)], dst_ref=window,
            send_sem=send_w.at[d - 1], recv_sem=recv_w,
            device_id={"cond": partner(ic, d, nc)}, device_id_type=MESH,
        )

    own_window = pltpu.make_async_copy(wave.at[pl.ds(0, 1)], window, local.at[5])

    @pl.when(ic == 0)
    def _():
        for d in range(nc - 1, 0, -1):
            window_copy(d).start()
        own_window.start()

    def exchange(axis, position, size, d, at, src, dst, send, recv):
        return pltpu.make_async_remote_copy(
            src_ref=src, dst_ref=dst.at[at],
            send_sem=send.at[d - 1], recv_sem=recv.at[d - 1],
            device_id={axis: partner(position, d, size)}, device_id_type=MESH,
        )

    def val_copies(d, at):
        return [
            exchange("val", iv, nv, d, at, gath_v.at[iv], gath_v, send_v, recv_v),
            exchange("val", iv, nv, d, at, gath_ve.at[iv], gath_ve, send_ve, recv_ve),
        ]

    def cond_copies(d, at):
        return [
            exchange("cond", ic, nc, d, at, gath_c.at[ic], gath_c, send_c, recv_c),
            exchange("cond", ic, nc, d, at, gath_ce.at[ic], gath_ce, send_ce, recv_ce),
        ]

    for d in range(nc - 1, 0, -1):
        for copy in cond_copies(d, ic):
            copy.start()
    for d in range(1, nv):
        for copy in val_copies(d, iv):
            copy.start()

    for block in range(own_wave.shape[0]):
        cos_x, sin_x, cos_p, sin_p = factors(own_wave[pl.ds(block, 1), :], points, 0.0)
        lanes = pl.ds(block * LANES, LANES)
        for plane in range(planes):
            at = pl.ds(plane * NG, NG)
            c, s = cos_p[plane:plane + 1, :], sin_p[plane:plane + 1, :]
            cos_rows[at, lanes] = (cos_x * c - sin_x * s).astype(jnp.bfloat16)
            sin_rows[at, lanes] = (sin_x * c + cos_x * s).astype(jnp.bfloat16)

    for d in range(1, nv):
        for copy in val_copies(d, source(iv, d, nv)):
            copy.wait_recv()

    count = group * cb
    height = nv * vb * count
    eye = lax.broadcasted_iota(jnp.int32, (cb, cb), 0) == lax.broadcasted_iota(jnp.int32, (cb, cb), 1)

    def fill(first):
        slot = first // group % slots
        orbitals, energies = [], []
        for d in range(first, first + group):
            at = source(ic, d, nc) if d else ic
            if d:
                for copy in cond_copies(d, at):
                    copy.wait_recv()
            orbitals.append(gath_c[at].astype(jnp.float32))
            row = jnp.broadcast_to(gath_ce[at].astype(jnp.float32), (cb, cb))
            column = jnp.sum(jnp.where(eye, row, 0.0), axis=1, keepdims=True)
            energies.append(jnp.broadcast_to(column, (cb, LANES)))
        orbitals = jnp.concatenate(orbitals, axis=0)

        def one_block(b, carry):
            block = gath_v[b].astype(jnp.float32)
            for v in range(vb):
                at = pl.ds(pl.multiple_of((b * vb + v) * count, count), count)
                dens[slot, at, :] = (orbitals * block[v:v + 1, :]).astype(jnp.bfloat16)
            return carry

        lax.fori_loop(0, nv, one_block, 0, unroll=nv <= 4)
        return jnp.concatenate(energies, axis=0)

    def use(first, energies):
        slot = first // group % slots
        weights = []
        for b in range(nv):
            block = gath_ve[b].astype(jnp.float32)
            for v in range(vb):
                own = jnp.broadcast_to(block[:, v:v + 1], (1, LANES))
                weights.append(1.0 / (energies - own))
        weighted = dot(dens[slot], window_table[...]) * jnp.concatenate(weights, axis=0)
        update = dot(split(jnp.transpose(weighted)[0:2 * rows]), dens[slot])
        update = update[0:2 * rows] + update[2 * rows:4 * rows]
        totals[...] = update if first == 0 else totals[...] + update

    ahead = min(2, slots, nc // group)
    energies = {}
    for step in range(ahead):
        energies[step] = fill(step * group)

    @pl.when(ic == 0)
    def _():
        own_window.wait()

    @pl.when(ic != 0)
    def _():
        window_copy(1).wait_recv()

    spread = jnp.broadcast_to(window[...], (8, LANES))
    first = pltpu.roll(spread, lax.rem(NW - iv * rows, NW), 1)
    lane = lax.broadcasted_iota(jnp.int32, (8, LANES), 1)
    index = jnp.where(lane < rows, first, pltpu.roll(first, rows, 1))[0:1, :]
    shift = jnp.where(lane < rows, 0.0, 3 * NG / 4)[0:1, :]
    cos_x, sin_x, cos_p, sin_p = factors(index, points, shift)
    for plane in range(planes):
        c, s = cos_p[plane:plane + 1, :], sin_p[plane:plane + 1, :]
        window_table[pl.ds(plane * NG, NG), :] = (cos_x * c - sin_x * s).astype(jnp.bfloat16)

    for step in range(nc // group):
        if step >= ahead:
            energies[step] = fill(step * group)
        use(step * group, energies.pop(step))

    cos_total = totals[0:rows, :]
    sin_total = totals[rows:2 * rows, :]
    by_cos = split(jnp.concatenate([cos_total, -sin_total], axis=0))
    by_sin = split(jnp.concatenate([sin_total, cos_total], axis=0))
    both = dot(by_cos, cos_rows[...]) + dot(by_sin, sin_rows[...])
    out[...] = both[0:2 * rows] + both[2 * rows:4 * rows]

    @pl.when(ic == 0)
    def _():
        for d in range(1, nc):
            window_copy(d).wait_send()

    for d in range(1, nc):
        for copy in cond_copies(d, ic):
            copy.wait_send()
    for d in range(1, nv):
        for copy in val_copies(d, iv):
            copy.wait_send()


def per_device(val_orbitals, cond_orbitals, val_energy, cond_energy, wave_index):
    nv, nc = lax.axis_size("val"), lax.axis_size("cond")
    vb, points = val_orbitals.shape
    cb = cond_orbitals.shape[0]
    count = wave_index.shape[0]
    rows = NW // nv
    group = 2 if nc % 2 == 0 else 1
    slots = min(4, nc // group)
    bf16, f32 = jnp.bfloat16, jnp.float32
    dma = pltpu.SemaphoreType.DMA
    out = pl.pallas_call(
        functools.partial(kernel, nv, nc, group, slots),
        out_shape=jax.ShapeDtypeStruct((2 * rows, count), f32),
        in_specs=[pl.BlockSpec(memory_space=pltpu.HBM)] * 5,
        out_specs=pl.BlockSpec(memory_space=pltpu.VMEM),
        scratch_shapes=[
            pltpu.VMEM((nv, vb, points), bf16),
            pltpu.VMEM((nc, cb, points), bf16),
            pltpu.VMEM((nv, 1, vb), bf16),
            pltpu.VMEM((nc, 1, cb), bf16),
            pltpu.VMEM((count // LANES, LANES), jnp.int32),
            pltpu.VMEM((1, LANES), jnp.int32),
            pltpu.VMEM((points, count), bf16),
            pltpu.VMEM((points, count), bf16),
            pltpu.VMEM((points, LANES), bf16),
            pltpu.VMEM((slots, nv * vb * group * cb, points), bf16),
            pltpu.VMEM((2 * rows, points), f32),
            dma((nv - 1,)), dma((nv - 1,)), dma((nc - 1,)), dma((nc - 1,)),
            dma((nv - 1,)), dma((nv - 1,)), dma((nc - 1,)), dma((nc - 1,)),
            dma((nc - 1,)), dma, dma((6,)),
        ],
        compiler_params=pltpu.CompilerParams(
            collective_id=0, has_side_effects=True, vmem_limit_bytes=VMEM_LIMIT
        ),
    )(*[
        pltpu.with_memory_space_constraint(value, pltpu.HBM)
        for value in (
            val_orbitals, cond_orbitals, val_energy.reshape(1, vb), cond_energy.reshape(1, cb),
            wave_index.reshape(count // LANES, LANES),
        )
    ])
    factor = -4.0 / math.sqrt(nv * vb * nc * cb)
    return factor * out[0:rows], factor * out[rows:2 * rows]


def solution(mesh):
    return jax.shard_map(
        per_device,
        mesh=mesh,
        in_specs=(P("val", None), P("cond", None), P("val"), P("cond"), P("cond")),
        out_specs=(P("val", "cond"), P("val", "cond")),
        check_vma=False,
    )
```

profile of v0, /device:TPU:0, one launch (start us, length us, event | category | flops | bytes accessed | tf_op | source)
XLA Modules:
  0.0 14.1 jit_solution(7623193935876282667)
XLA Ops:
  0.6 12.8 %shard_map.68 = f32[64,512]{1,0:T(8,128)S(1)} custom-call(bf16[4,768]{1,0:T(4,128)(2,1)} %val.1, bf16[8,768]{1,0:T(8,128)(2,1)} %cond.1, bf16[1,4]{1,0:T(2,128)(2,1)} %bitcast.4, bf16[1,8]{1,0:T(2,128)(2,1)} %bitcast.5, s32[4,128]{1,0:T(4,128)} %bitcast.3), custom_call_target="tpu_custom_call" | custom-call | tf_op jit(solution)/shard_map/pallas_call | solution.py:273
  13.4 0.7 %slice_multiply_fusion = (f32[32,512]{1,0:T(8,128)}, f32[32,512]{1,0:T(8,128)}) fusion(f32[64,512]{1,0:T(8,128)S(1)} %shard_map.68), kind=kLoop, calls=%fused_computation | loop fusion | flops 32768 | bytes 262144 | tf_op jit(solution)/shard_map/mul | solution.py:305
where the time goes:
time: 14.2 us; the launch traced here: 14.1 us
  Pallas kernels  12.8 us (90%)
  other arithmetic  0.66 us (5%)
  between operations  0.64 us (5%)
    pallas_call x1, Pallas kernels, per_device(): pl.pallas_call(functools.partial(kernel, nv, nc, group, slots), out_shape...  12.8 us
    mul x1, other arithmetic, per_device(): return (factor * out[0:rows], factor * out[rows:2 * rows])  0.66 us

commit v1 on v0

v1 whole, which is shorter than its diff:
```python
import functools
import math

import jax
import jax.numpy as jnp
from jax import lax
from jax.experimental import pallas as pl
from jax.experimental.pallas import tpu as pltpu
from jax.sharding import PartitionSpec as P

NG = 96
NW = 128
SLAB_Y = 4
LANES = 128
VMEM_LIMIT = 24 * 1024 * 1024
MESH = pl.DeviceIdType.MESH


def modulo(value, period):
    return value - period * jnp.floor((value + 0.5) * (1.0 / period))


def cos_turns(turns):
    angle = (turns - NG / 2) * (math.pi / NG)
    square = angle * angle
    series = 1.0
    for order in (10, 8, 6, 4, 2):
        series = 1.0 - square * series * (1.0 / (order * (order + 1)))
    sine = angle * series
    return 2.0 * sine * sine - 1.0


def wave_parts(flat):
    wave_x = jnp.floor((flat + 0.5) * (1.0 / (NG * NG)))
    rest = flat - wave_x * (NG * NG)
    wave_y = jnp.floor((rest + 0.5) * (1.0 / NG))
    return wave_x, wave_y, rest - wave_y * NG


def point_parts(point):
    plane = jnp.floor((point + 0.5) * (1.0 / NG))
    along_z = jnp.floor((plane + 0.5) * (1.0 / SLAB_Y))
    return point - plane * NG, plane - along_z * SLAB_Y, along_z


def iota(shape, axis):
    return lax.broadcasted_iota(jnp.int32, shape, axis).astype(jnp.float32)


def factors(index, points):
    wave_x, wave_y, wave_z = wave_parts(index.astype(jnp.float32))
    planes = points // NG
    along_x = iota((NG, LANES), 0)
    plane = iota((planes, LANES), 0)
    along_z = jnp.floor((plane + 0.5) * (1.0 / SLAB_Y))
    along_y = plane - along_z * SLAB_Y
    turns_x = modulo(along_x * wave_x, NG)
    turns_yz = modulo(along_y * wave_y + along_z * wave_z, NG)
    quarter = 3 * NG // 4
    return (
        cos_turns(turns_x),
        cos_turns(modulo(turns_x + quarter, NG)),
        cos_turns(turns_yz),
        cos_turns(modulo(turns_yz + quarter, NG)),
    )


def split(value):
    high = value.astype(jnp.bfloat16)
    low = (value - high.astype(jnp.float32)).astype(jnp.bfloat16)
    return jnp.concatenate([high, low], axis=0)


def dot(left, right):
    return jnp.dot(left, right, preferred_element_type=jnp.float32)


def dot_t(left, right):
    return lax.dot_general(left, right, (((1,), (1,)), ((), ())), preferred_element_type=jnp.float32)


def flip(position, size):
    if size % 2:
        return position
    return position + 1 - 2 * lax.rem(position, 2)


def nearest(position, step, size):
    both = jnp.minimum(position, size - 1 - position)
    half = (step + 1) // 2
    near = position + half if step % 2 else position - half
    side = jnp.where(position < size - 1 - position, 1, -1)
    return jnp.where(step <= 2 * both, near, position + side * (step - both))


def kernel(
    nv, nc, group, slots,
    val, cond, val_energy, cond_energy, wave, out,
    gath_v, gath_c, gath_ve, gath_ce, own_wave, window, cos_rows, sin_rows, window_table, dens, weights, totals,
    recv_v, recv_ve, recv_c, recv_ce, recv_w, send, ready_c, ready_v, local,
):
    iv = lax.axis_index("val")
    ic = lax.axis_index("cond")
    vb, points = val.shape
    cb = cond.shape[0]
    rows = NW // nv
    planes = points // NG
    steps = nc // group
    mine = ic // group
    rank = flip(iv, nv)

    barrier = pltpu.get_barrier_semaphore()

    def each(first, last, body):
        def step(j, carry):
            body(j)
            return carry

        lax.fori_loop(first, last, step, 0)

    def greet(axis, peer):
        pl.semaphore_signal(barrier, inc=1, device_id={axis: peer}, device_id_type=MESH)

    each(ic + 1, nc, lambda j: greet("cond", j))
    each(rank + 1, nv, lambda j: greet("val", flip(j, nv)))

    wave_copy = pltpu.make_async_copy(wave, own_wave, local.at[0])
    own_copies = [
        pltpu.make_async_copy(cond, gath_c.at[ic], local.at[1]),
        pltpu.make_async_copy(val, gath_v.at[iv], local.at[2]),
        pltpu.make_async_copy(cond_energy, gath_ce.at[ic], local.at[3]),
        pltpu.make_async_copy(val_energy, gath_ve.at[iv], local.at[4]),
    ]
    wave_copy.start()
    for copy in own_copies:
        copy.start()

    def remote(axis, peer, src, dst, send_sem, recv_sem):
        return pltpu.make_async_remote_copy(
            src_ref=src, dst_ref=dst, send_sem=send_sem, recv_sem=recv_sem,
            device_id={axis: peer}, device_id_type=MESH,
        )

    def send_cond(peer):
        remote("cond", peer, cond, gath_c.at[ic], send.at[0], recv_c.at[mine]).start()
        remote("cond", peer, cond_energy, gath_ce.at[ic], send.at[1], recv_ce.at[mine]).start()

    def send_val(peer):
        remote("val", peer, val, gath_v.at[iv], send.at[2], recv_v).start()
        remote("val", peer, val_energy, gath_ve.at[iv], send.at[3], recv_ve).start()

    def wait_for(part, semaphore):
        pltpu.make_async_copy(part, part, semaphore).wait()

    @pl.when(ic + rank > 0)
    def _():
        pl.semaphore_wait(barrier, ic + rank)

    each(0, ic, lambda j: pl.semaphore_signal(
        ready_c.at[mine], inc=1, device_id={"cond": j}, device_id_type=MESH))
    each(0, rank, lambda j: pl.semaphore_signal(
        ready_v, inc=1, device_id={"val": flip(j, nv)}, device_id_type=MESH))
    each(0, ic, send_cond)
    each(0, rank, lambda j: send_val(flip(j, nv)))

    wave_copy.wait()
    for block in range(own_wave.shape[0]):
        cos_x, sin_x, cos_p, sin_p = factors(own_wave[pl.ds(block, 1), :], points)
        lanes = pl.ds(block * LANES, LANES)
        for plane in range(planes):
            at = pl.ds(plane * NG, NG)
            c, s = cos_p[plane:plane + 1, :], sin_p[plane:plane + 1, :]
            cos_rows[at, lanes] = (cos_x * c - sin_x * s).astype(jnp.bfloat16)
            sin_rows[at, lanes] = (sin_x * c + cos_x * s).astype(jnp.bfloat16)

    def window_to(peer):
        @pl.when(ic == 0)
        def _():
            remote("cond", peer, own_wave.at[pl.ds(0, 1)], window, send.at[4], recv_w).start()

    own_window = pltpu.make_async_copy(wave.at[pl.ds(0, 1)], window, local.at[0])

    @pl.when(ic == 0)
    def _():
        own_window.start()

    @pl.when(rank < nv - 1)
    def _():
        pl.semaphore_wait(ready_v, nv - 1 - rank)

    each(rank + 1, nv, lambda j: send_val(flip(j, nv)))

    if group == 2:
        @pl.when(lax.rem(ic, 2) == 0)
        def _():
            pl.semaphore_wait(ready_c.at[mine], 1)
            window_to(ic + 1)
            send_cond(ic + 1)

    def serve(step):
        other = nearest(mine, step, steps)

        @pl.when(other > mine)
        def _():
            pl.semaphore_wait(ready_c.at[other], group)
            for j in range(group):
                window_to(other * group + j)
            for j in range(group):
                send_cond(other * group + j)

    if steps > 1:
        serve(1)
    for copy in own_copies:
        copy.wait()
    wait_for(gath_v.at[pl.ds(0, nv - 1)], recv_v)
    wait_for(gath_ve.at[pl.ds(0, nv - 1)], recv_ve)

    count = group * cb
    height = nv * vb * count
    pair = iota((1, height), 1)
    pair_v = jnp.floor((pair + 0.5) * (1.0 / count))
    pair_c = pair - pair_v * count

    def spread(row, length, index, offset):
        square = jnp.broadcast_to(row.astype(jnp.float32), (length, length))
        eye = iota((length, length), 0) == iota((length, length), 1)
        column = jnp.sum(jnp.where(eye, square, 0.0), axis=1, keepdims=True)
        chosen = iota((length, height), 0) + offset == index
        return jnp.sum(jnp.where(chosen, column, 0.0), axis=0, keepdims=True)

    own_val = sum(spread(gath_ve[b], vb, pair_v, b * vb) for b in range(nv))

    def fill(step):
        slot = step % slots
        if step:
            other = nearest(mine, step, steps)
            wait_for(gath_c.at[pl.ds(other * group, group)], recv_c.at[other])
            wait_for(gath_ce.at[pl.ds(other * group, group)], recv_ce.at[other])
        else:
            other = mine
            if group == 2:
                wait_for(gath_c.at[flip(ic, nc)], recv_c.at[mine])
                wait_for(gath_ce.at[flip(ic, nc)], recv_ce.at[mine])
        at = [other * group + j for j in range(group)]
        orbitals = jnp.concatenate([gath_c[j] for j in at], axis=0)
        own_cond = sum(spread(gath_ce[j], cb, pair_c, n * cb) for n, j in enumerate(at))
        weights[0:1, slot * height:(slot + 1) * height] = 1.0 / (own_cond - own_val)

        def one_block(b, carry):
            block = gath_v[b]
            for v in range(vb):
                first = pl.multiple_of(slot * height + (b * vb + v) * count, count)
                dens[pl.ds(first, count), :] = orbitals * block[v:v + 1, :]
            return carry

        lax.fori_loop(0, nv, one_block, 0, unroll=nv <= 4)

    def use(step, span):
        slot = step % slots
        at = pl.ds(slot * height, span * height)
        weighted = dot_t(window_table[...], dens[at, :]) * weights[0:1, slot * height:(slot + span) * height]
        update = dot(split(weighted), dens[at, :])
        update = update[0:2 * rows] + update[2 * rows:4 * rows]
        totals[...] = update if step == 0 else totals[...] + update

    fill(0)
    for step in range(2, steps):
        serve(step)
    if steps > 1:
        fill(1)

    @pl.when(ic == 0)
    def _():
        own_window.wait()

    @pl.when(ic != 0)
    def _():
        wait_for(window, recv_w)

    spread_wave = jnp.broadcast_to(window[...], (8, LANES))
    first = pltpu.roll(spread_wave, lax.rem(NW - iv * rows, NW), 1)
    lane = lax.broadcasted_iota(jnp.int32, (8, LANES), 1)
    index = jnp.where(lane < rows, first, pltpu.roll(first, rows, 1))[0:1, :].astype(jnp.float32)
    index = jnp.transpose(jnp.broadcast_to(index, (LANES, LANES)))[0:2 * rows]
    wave_x, wave_y, wave_z = wave_parts(index)
    shift = jnp.where(iota((2 * rows, LANES), 0) < rows, 0.0, 3 * NG / 4)
    for block in range(points // LANES):
        along_x, along_y, along_z = point_parts(iota((1, LANES), 1) + block * LANES)
        turns = modulo(wave_x * along_x + wave_y * along_y + wave_z * along_z + shift, NG)
        window_table[:, pl.ds(block * LANES, LANES)] = cos_turns(turns).astype(jnp.bfloat16)

    begun = min(2, steps)
    use(0, begun)
    for step in range(begun, steps):
        fill(step)
        use(step, 1)

    sums = split(totals[...])
    by_cos = dot(sums, cos_rows[...])
    by_sin = dot(sums, sin_rows[...])
    by_cos = by_cos[0:2 * rows] + by_cos[2 * rows:4 * rows]
    by_sin = by_sin[0:2 * rows] + by_sin[2 * rows:4 * rows]
    out[0:rows, :] = by_cos[0:rows] + by_sin[rows:2 * rows]
    out[rows:2 * rows, :] = by_sin[0:rows] - by_cos[rows:2 * rows]

    wait_for(gath_c.at[pl.ds(0, nc - 1)], send.at[0])
    wait_for(gath_ce.at[pl.ds(0, nc - 1)], send.at[1])
    wait_for(gath_v.at[pl.ds(0, nv - 1)], send.at[2])
    wait_for(gath_ve.at[pl.ds(0, nv - 1)], send.at[3])

    @pl.when(ic == 0)
    def _():
        each(1, nc, lambda j: wait_for(window, send.at[4]))


def per_device(val_orbitals, cond_orbitals, val_energy, cond_energy, wave_index):
    nv, nc = lax.axis_size("val"), lax.axis_size("cond")
    vb, points = val_orbitals.shape
    cb = cond_orbitals.shape[0]
    count = wave_index.shape[0]
    rows = NW // nv
    group = 2 if nc % 2 == 0 else 1
    steps = nc // group
    slots = min(4, steps)
    height = nv * vb * group * cb
    bf16, f32 = jnp.bfloat16, jnp.float32
    dma = pltpu.SemaphoreType.DMA
    regular = pltpu.SemaphoreType.REGULAR
    out = pl.pallas_call(
        functools.partial(kernel, nv, nc, group, slots),
        out_shape=jax.ShapeDtypeStruct((2 * rows, count), f32),
        in_specs=[pl.BlockSpec(memory_space=pltpu.HBM)] * 5,
        out_specs=pl.BlockSpec(memory_space=pltpu.VMEM),
        scratch_shapes=[
            pltpu.VMEM((nv, vb, points), bf16),
            pltpu.VMEM((nc, cb, points), bf16),
            pltpu.VMEM((nv, 1, vb), bf16),
            pltpu.VMEM((nc, 1, cb), bf16),
            pltpu.VMEM((count // LANES, LANES), jnp.int32),
            pltpu.VMEM((1, LANES), jnp.int32),
            pltpu.VMEM((points, count), bf16),
            pltpu.VMEM((points, count), bf16),
            pltpu.VMEM((2 * rows, points), bf16),
            pltpu.VMEM((slots * height, points), bf16),
            pltpu.VMEM((8, slots * height), f32),
            pltpu.VMEM((2 * rows, points), f32),
            dma, dma, dma((steps,)), dma((steps,)), dma, dma((5,)), regular((steps,)), regular, dma((5,)),
        ],
        compiler_params=pltpu.CompilerParams(
            collective_id=0, has_side_effects=True, vmem_limit_bytes=VMEM_LIMIT
        ),
    )(*[
        pltpu.with_memory_space_constraint(value, pltpu.HBM)
        for value in (
            val_orbitals, cond_orbitals, val_energy.reshape(1, vb), cond_energy.reshape(1, cb),
            wave_index.reshape(count // LANES, LANES),
        )
    ])
    factor = -4.0 / math.sqrt(nv * vb * nc * cb)
    return factor * out[0:rows], factor * out[rows:2 * rows]


def solution(mesh):
    return jax.shard_map(
        per_device,
        mesh=mesh,
        in_specs=(P("val", None), P("cond", None), P("val"), P("cond"), P("cond")),
        out_specs=(P("val", "cond"), P("val", "cond")),
        check_vma=False,
    )
```

time: 14.2 us -> 11.9 us (0.84)
  the two profiles are of different devices: /device:TPU:0 before, /device:TPU:24 now
where the time goes in v1:
time: 11.9 us; the launch traced here: 11.7 us
  Pallas kernels  10.4 us (87%)
  other arithmetic  0.66 us (6%)
  between operations  0.64 us (5%)
    pallas_call x1, Pallas kernels, per_device(): pl.pallas_call(functools.partial(kernel, nv, nc, group, slots), out_shape...  10.4 us
    mul x1, other arithmetic, per_device(): return (factor * out[0:rows], factor * out[rows:2 * rows])  0.66 us

profile of v1, /device:TPU:24, one launch (start us, length us, event | category | flops | bytes accessed | tf_op | source)
XLA Modules:
  0.0 11.7 jit_solution(12673160349718904813)
XLA Ops:
  0.6 10.4 %shard_map.68 = f32[64,512]{1,0:T(8,128)S(1)} custom-call(bf16[4,768]{1,0:T(4,128)(2,1)} %val.1, bf16[8,768]{1,0:T(8,128)(2,1)} %cond.1, bf16[1,4]{1,0:T(2,128)(2,1)} %bitcast.4, bf16[1,8]{1,0:T(2,128)(2,1)} %bitcast.5, s32[4,128]{1,0:T(4,128)} %bitcast.3), custom_call_target="tpu_custom_call" | custom-call | tf_op jit(solution)/shard_map/pallas_call | solution.py:329
  11.1 0.7 %slice_multiply_fusion = (f32[32,512]{1,0:T(8,128)}, f32[32,512]{1,0:T(8,128)}) fusion(f32[64,512]{1,0:T(8,128)S(1)} %shard_map.68), kind=kLoop, calls=%fused_computation | loop fusion | flops 32768 | bytes 262144 | tf_op jit(solution)/shard_map/mul | solution.py:360

commit v2 on v1

v2 whole, which is shorter than its diff:
```python
import functools
import math

import jax
import jax.numpy as jnp
from jax import lax
from jax.experimental import pallas as pl
from jax.experimental.pallas import tpu as pltpu
from jax.sharding import PartitionSpec as P

NG = 96
NW = 128
SLAB_Y = 4
LANES = 128
VMEM_LIMIT = 24 * 1024 * 1024
MESH = pl.DeviceIdType.MESH


def modulo(value, period):
    return value - period * jnp.floor((value + 0.5) * (1.0 / period))


def cos_turns(turns):
    angle = (turns - NG / 2) * (math.pi / NG)
    square = angle * angle
    series = 1.0
    for order in (10, 8, 6, 4, 2):
        series = 1.0 - square * series * (1.0 / (order * (order + 1)))
    sine = angle * series
    return 2.0 * sine * sine - 1.0


def wave_parts(flat):
    wave_x = jnp.floor((flat + 0.5) * (1.0 / (NG * NG)))
    rest = flat - wave_x * (NG * NG)
    wave_y = jnp.floor((rest + 0.5) * (1.0 / NG))
    return wave_x, wave_y, rest - wave_y * NG


def point_parts(point):
    plane = jnp.floor((point + 0.5) * (1.0 / NG))
    along_z = jnp.floor((plane + 0.5) * (1.0 / SLAB_Y))
    return point - plane * NG, plane - along_z * SLAB_Y, along_z


def iota(shape, axis):
    return lax.broadcasted_iota(jnp.int32, shape, axis).astype(jnp.float32)


def factors(index, points):
    wave_x, wave_y, wave_z = wave_parts(index.astype(jnp.float32))
    planes = points // NG
    along_x = iota((NG, LANES), 0)
    plane = iota((planes, LANES), 0)
    along_z = jnp.floor((plane + 0.5) * (1.0 / SLAB_Y))
    along_y = plane - along_z * SLAB_Y
    turns_x = modulo(along_x * wave_x, NG)
    turns_yz = modulo(along_y * wave_y + along_z * wave_z, NG)
    quarter = 3 * NG // 4
    return (
        cos_turns(turns_x),
        cos_turns(modulo(turns_x + quarter, NG)),
        cos_turns(turns_yz),
        cos_turns(modulo(turns_yz + quarter, NG)),
    )


def split(value):
    high = value.astype(jnp.bfloat16)
    low = (value - high.astype(jnp.float32)).astype(jnp.bfloat16)
    return jnp.concatenate([high, low], axis=0)


def dot(left, right):
    return jnp.dot(left, right, preferred_element_type=jnp.float32)


def dot_t(left, right):
    return lax.dot_general(left, right, (((1,), (1,)), ((), ())), preferred_element_type=jnp.float32)


def flip(position, size):
    if size % 2:
        return position
    return position + 1 - 2 * lax.rem(position, 2)


def nearest(position, step, size):
    both = jnp.minimum(position, size - 1 - position)
    half = (step + 1) // 2
    near = position + half if step % 2 else position - half
    side = jnp.where(position < size - 1 - position, 1, -1)
    return jnp.where(step <= 2 * both, near, position + side * (step - both))


def kernel(
    nv, nc, slots,
    val, cond, val_energy, cond_energy, wave, out,
    gath_v, gath_c, gath_ve, gath_ce, own_wave, window, cos_rows, sin_rows, window_table, dens, weights, totals,
    recv_v, recv_ve, recv_c, recv_ce, recv_w, send, ready, local,
):
    iv = lax.axis_index("val")
    ic = lax.axis_index("cond")
    vb, points = val.shape
    cb = cond.shape[0]
    rows = NW // nv
    planes = points // NG
    steps = nc // 2
    mine = ic // 2
    core = lax.rem(iv, 2)
    hub = iv - core
    scout = hub + 1
    is_hub = core == 0
    is_scout = core == 1

    barrier = pltpu.get_barrier_semaphore()

    def each(first, last, body):
        def step(j, carry):
            body(j)
            return carry

        lax.fori_loop(first, last, step, 0)

    def signal(semaphore, v, c):
        pl.semaphore_signal(semaphore, inc=1, device_id={"val": v, "cond": c}, device_id_type=MESH)

    @pl.when(ic == 0)
    def _():
        each(1, nc, lambda j: signal(barrier, scout, nc - j))

    @pl.when(ic > 0)
    def _():
        each(ic + 1, nc, lambda j: signal(barrier, hub, j))

    @pl.when(is_scout)
    def _():
        signal(barrier, hub, ic)

    each(1, nv // 2, lambda k: signal(barrier, lax.rem(hub + 2 * k, nv), ic))

    wave_copy = pltpu.make_async_copy(wave, own_wave, local.at[0])
    own_copies = [
        pltpu.make_async_copy(cond, gath_c.at[ic], local.at[1]),
        pltpu.make_async_copy(val, gath_v.at[iv], local.at[2]),
        pltpu.make_async_copy(cond_energy, gath_ce.at[ic], local.at[3]),
        pltpu.make_async_copy(val_energy, gath_ve.at[iv], local.at[4]),
    ]
    wave_copy.start()
    for copy in own_copies:
        copy.start()

    def remote(v, c, src, dst, semaphore):
        pltpu.make_async_remote_copy(
            src_ref=src, dst_ref=dst, send_sem=send, recv_sem=semaphore,
            device_id={"val": v, "cond": c}, device_id_type=MESH,
        ).start()

    def send_cond(v, c):
        remote(v, c, cond, gath_c.at[ic], recv_c.at[mine])
        remote(v, c, cond_energy, gath_ce.at[ic], recv_ce.at[mine])

    def send_val():
        def one(k):
            peer = lax.rem(iv + k, nv)
            remote(peer, ic, val, gath_v.at[iv], recv_v)
            remote(peer, ic, val_energy, gath_ve.at[iv], recv_ve)

        each(1, nv, one)

    def send_origin(v, c, source, first, count):
        part, energies = gath_c.at[pl.ds(first, count)], gath_ce.at[pl.ds(first, count)]
        remote(v, c, source, window, recv_w)
        remote(v, c, part, part, recv_c.at[0])
        remote(v, c, energies, energies, recv_ce.at[0])

    def wait_for(part, semaphore):
        pltpu.make_async_copy(part, part, semaphore).wait()

    @pl.when(is_scout & (ic > 0))
    def _():
        pl.semaphore_wait(barrier, 2)
        signal(ready.at[ic], scout, 0)
        send_cond(hub, 0)
        send_cond(scout, 0)

    @pl.when(is_hub)
    def _():
        pl.semaphore_wait(barrier, nv - 1 + 2 * jnp.maximum(ic - 1, 0))
        signal(ready.at[ic], scout, ic)
        each(2, ic, lambda j: signal(ready.at[ic], hub, j))

        def both(j):
            send_cond(hub, j)
            send_cond(scout, j)

        each(1, ic, both)
        send_val()

    wave_copy.wait()
    for block in range(own_wave.shape[0]):
        cos_x, sin_x, cos_p, sin_p = factors(own_wave[pl.ds(block, 1), :], points)
        lanes = pl.ds(block * LANES, LANES)
        for plane in range(planes):
            at = pl.ds(plane * NG, NG)
            c, s = cos_p[plane:plane + 1, :], sin_p[plane:plane + 1, :]
            cos_rows[at, lanes] = (cos_x * c - sin_x * s).astype(jnp.bfloat16)
            sin_rows[at, lanes] = (sin_x * c + cos_x * s).astype(jnp.bfloat16)
    for copy in own_copies:
        copy.wait()

    @pl.when(is_scout)
    def _():
        pl.semaphore_wait(ready.at[ic], 1)
        send_val()

    def wait_origin(first, count):
        wait_for(gath_c.at[pl.ds(first, count)], recv_c.at[0])
        wait_for(gath_ce.at[pl.ds(first, count)], recv_ce.at[0])

    own_window = own_wave.at[pl.ds(0, 1)]

    @pl.when(is_scout & (ic == 0))
    def _():
        pl.semaphore_wait(ready.at[1], 1)
        send_origin(scout, 1, own_window, 0, 1)
        wait_origin(1, 1)

        def serve(j):
            pl.semaphore_wait(ready.at[j], 1)
            send_origin(scout, j, own_window, 0, 2)

        each(2, nc, serve)

    @pl.when(is_hub & (ic > 1))
    def _():
        def serve(j):
            pl.semaphore_wait(ready.at[j], 1)
            send_cond(hub, j)
            send_cond(scout, j)

        each(ic + 1, nc, serve)

    @pl.when(ic == 0)
    def _():
        copy = pltpu.make_async_copy(own_window, window, local.at[0])
        copy.start()
        copy.wait()

    @pl.when(is_hub & (ic == 0))
    def _():
        wait_origin(1, 1)

    @pl.when(ic > 0)
    def _():
        wait_for(window, recv_w)

    @pl.when(ic == 1)
    def _():
        wait_origin(0, 1)

    @pl.when(ic > 1)
    def _():
        wait_origin(0, 2)

    @pl.when(is_scout & (ic == 1))
    def _():
        send_origin(hub, ic, window, 0, 1)

    @pl.when(is_scout & (ic > 1))
    def _():
        send_origin(hub, ic, window, 0, 2)

    spread_wave = jnp.broadcast_to(window[...], (8, LANES))
    first = pltpu.roll(spread_wave, lax.rem(NW - iv * rows, NW), 1)
    lane = lax.broadcasted_iota(jnp.int32, (8, LANES), 1)
    index = jnp.where(lane < rows, first, pltpu.roll(first, rows, 1))[0:1, :].astype(jnp.float32)
    index = jnp.transpose(jnp.broadcast_to(index, (LANES, LANES)))[0:2 * rows]
    wave_x, wave_y, wave_z = wave_parts(index)
    shift = jnp.where(iota((2 * rows, LANES), 0) < rows, 0.0, 3 * NG / 4)
    for block in range(points // LANES):
        along_x, along_y, along_z = point_parts(iota((1, LANES), 1) + block * LANES)
        turns = modulo(wave_x * along_x + wave_y * along_y + wave_z * along_z + shift, NG)
        window_table[:, pl.ds(block * LANES, LANES)] = cos_turns(turns).astype(jnp.bfloat16)

    wait_for(gath_v.at[pl.ds(0, nv - 1)], recv_v)
    wait_for(gath_ve.at[pl.ds(0, nv - 1)], recv_ve)

    count = 2 * cb
    height = nv * vb * count
    pair = iota((1, height), 1)
    pair_v = jnp.floor((pair + 0.5) * (1.0 / count))
    pair_c = pair - pair_v * count

    def spread(row, length, index, offset):
        square = jnp.broadcast_to(row.astype(jnp.float32), (length, length))
        eye = iota((length, length), 0) == iota((length, length), 1)
        column = jnp.sum(jnp.where(eye, square, 0.0), axis=1, keepdims=True)
        chosen = iota((length, height), 0) + offset == index
        return jnp.sum(jnp.where(chosen, column, 0.0), axis=0, keepdims=True)

    own_val = sum(spread(gath_ve[b], vb, pair_v, b * vb) for b in range(nv))

    def fill(step):
        slot = step % slots
        if step == 0:
            other = mine
            peer = flip(ic, nc)

            @pl.when(mine > 0)
            def _():
                wait_for(gath_c.at[peer], recv_c.at[mine])
                wait_for(gath_ce.at[peer], recv_ce.at[mine])
        else:
            other = nearest(mine, step, steps)
            if step == 1:
                other = jnp.where(mine > 0, 0, other)
            else:
                other = jnp.where(mine > 0, nearest(mine - 1, step - 1, steps - 1) + 1, other)

            @pl.when(other > 0)
            def _():
                wait_for(gath_c.at[pl.ds(other * 2, 2)], recv_c.at[other])
                wait_for(gath_ce.at[pl.ds(other * 2, 2)], recv_ce.at[other])
        at = [other * 2, other * 2 + 1]
        orbitals = jnp.concatenate([gath_c[j] for j in at], axis=0)
        own_cond = sum(spread(gath_ce[j], cb, pair_c, n * cb) for n, j in enumerate(at))
        weights[0:1, slot * height:(slot + 1) * height] = 1.0 / (own_cond - own_val)

        def one_block(b, carry):
            block = gath_v[b]
            for v in range(vb):
                first = pl.multiple_of(slot * height + (b * vb + v) * count, count)
                dens[pl.ds(first, count), :] = orbitals * block[v:v + 1, :]
            return carry

        lax.fori_loop(0, nv, one_block, 0, unroll=nv <= 4)

    def use(step, span):
        slot = step % slots
        at = pl.ds(slot * height, span * height)
        weighted = dot_t(window_table[...], dens[at, :]) * weights[0:1, slot * height:(slot + span) * height]
        update = dot(split(weighted), dens[at, :])
        update = update[0:2 * rows] + update[2 * rows:4 * rows]
        totals[...] = update if step == 0 else totals[...] + update

    for step in range(0, steps, 2):
        span = min(2, steps - step)
        for n in range(span):
            fill(step + n)
        use(step, span)

    sums = split(totals[...])
    by_cos = dot(sums, cos_rows[...])
    by_sin = dot(sums, sin_rows[...])
    by_cos = by_cos[0:2 * rows] + by_cos[2 * rows:4 * rows]
    by_sin = by_sin[0:2 * rows] + by_sin[2 * rows:4 * rows]
    out[0:rows, :] = by_cos[0:rows] + by_sin[rows:2 * rows]
    out[rows:2 * rows, :] = by_sin[0:rows] - by_cos[rows:2 * rows]

    def sent(conds, windows):
        def one(j):
            wait_for(gath_c.at[0], send)
            wait_for(gath_ce.at[0], send)

        each(0, conds, one)
        each(0, windows, lambda j: wait_for(window, send))

    wait_for(gath_v.at[pl.ds(0, nv - 1)], send)
    wait_for(gath_ve.at[pl.ds(0, nv - 1)], send)

    @pl.when(is_hub & (ic > 1))
    def _():
        sent(2 * (nc - 2), 0)

    @pl.when(is_scout & (ic == 0))
    def _():
        sent(1 + 2 * (nc - 2), nc - 1)

    @pl.when(is_scout & (ic == 1))
    def _():
        sent(3, 1)

    @pl.when(is_scout & (ic > 1))
    def _():
        sent(4, 1)


def per_device(val_orbitals, cond_orbitals, val_energy, cond_energy, wave_index):
    nv, nc = lax.axis_size("val"), lax.axis_size("cond")
    vb, points = val_orbitals.shape
    cb = cond_orbitals.shape[0]
    count = wave_index.shape[0]
    rows = NW // nv
    steps = nc // 2
    slots = min(4, steps)
    height = nv * vb * 2 * cb
    bf16, f32 = jnp.bfloat16, jnp.float32
    dma = pltpu.SemaphoreType.DMA
    regular = pltpu.SemaphoreType.REGULAR
    out = pl.pallas_call(
        functools.partial(kernel, nv, nc, slots),
        out_shape=jax.ShapeDtypeStruct((2 * rows, count), f32),
        in_specs=[pl.BlockSpec(memory_space=pltpu.HBM)] * 5,
        out_specs=pl.BlockSpec(memory_space=pltpu.VMEM),
        scratch_shapes=[
            pltpu.VMEM((nv, vb, points), bf16),
            pltpu.VMEM((nc, cb, points), bf16),
            pltpu.VMEM((nv, 1, vb), bf16),
            pltpu.VMEM((nc, 1, cb), bf16),
            pltpu.VMEM((count // LANES, LANES), jnp.int32),
            pltpu.VMEM((1, LANES), jnp.int32),
            pltpu.VMEM((points, count), bf16),
            pltpu.VMEM((points, count), bf16),
            pltpu.VMEM((2 * rows, points), bf16),
            pltpu.VMEM((slots * height, points), bf16),
            pltpu.VMEM((8, slots * height), f32),
            pltpu.VMEM((2 * rows, points), f32),
            dma, dma, dma((steps,)), dma((steps,)), dma, dma, regular((nc,)), dma((5,)),
        ],
        compiler_params=pltpu.CompilerParams(
            collective_id=0, has_side_effects=True, vmem_limit_bytes=VMEM_LIMIT
        ),
    )(*[
        pltpu.with_memory_space_constraint(value, pltpu.HBM)
        for value in (
            val_orbitals, cond_orbitals, val_energy.reshape(1, vb), cond_energy.reshape(1, cb),
            wave_index.reshape(count // LANES, LANES),
        )
    ])
    factor = -4.0 / math.sqrt(nv * vb * nc * cb)
    return factor * out[0:rows], factor * out[rows:2 * rows]


def solution(mesh):
    return jax.shard_map(
        per_device,
        mesh=mesh,
        in_specs=(P("val", None), P("cond", None), P("val"), P("cond"), P("cond")),
        out_specs=(P("val", "cond"), P("val", "cond")),
        check_vma=False,
    )
```

time: 11.9 us -> 11.1 us (0.933)
  the two profiles are of different devices: /device:TPU:24 before, /device:TPU:30 now
where the time goes in v2:
time: 11.1 us; the launch traced here: 11 us
  Pallas kernels  9.68 us (87%)
  other arithmetic  0.66 us (6%)
  between operations  0.64 us (6%)
    pallas_call x1, Pallas kernels, per_device(): pl.pallas_call(functools.partial(kernel, nv, nc, slots), out_shape=jax.Sh...  9.68 us
    mul x1, other arithmetic, per_device(): return (factor * out[0:rows], factor * out[rows:2 * rows])  0.66 us

profile of v2, /device:TPU:30, one launch (start us, length us, event | category | flops | bytes accessed | tf_op | source)
XLA Modules:
  0.0 11.0 jit_solution(4105260274997068210)
XLA Ops:
  0.6 9.7 %shard_map.68 = f32[64,512]{1,0:T(8,128)S(1)} custom-call(bf16[4,768]{1,0:T(4,128)(2,1)} %val.1, bf16[8,768]{1,0:T(8,128)(2,1)} %cond.1, bf16[1,4]{1,0:T(2,128)(2,1)} %bitcast.4, bf16[1,8]{1,0:T(2,128)(2,1)} %bitcast.5, s32[4,128]{1,0:T(4,128)} %bitcast.3), custom_call_target="tpu_custom_call" | custom-call | tf_op jit(solution)/shard_map/pallas_call | solution.py:401
  10.3 0.7 %slice_multiply_fusion = (f32[32,512]{1,0:T(8,128)}, f32[32,512]{1,0:T(8,128)}) fusion(f32[64,512]{1,0:T(8,128)S(1)} %shard_map.68), kind=kLoop, calls=%fused_computation | loop fusion | flops 32768 | bytes 262144 | tf_op jit(solution)/shard_map/mul | solution.py:432

commit v3 on v2

--- a/solution.py
+++ b/solution.py
@@ -97,7 +97,7 @@
     nv, nc, slots,
     val, cond, val_energy, cond_energy, wave, out,
     gath_v, gath_c, gath_ve, gath_ce, own_wave, window, cos_rows, sin_rows, window_table, dens, weights, totals,
-    recv_v, recv_ve, recv_c, recv_ce, recv_w, send, ready, local,
+    recv_v, recv_ve, recv_c, recv_ce, recv_w, send, ready, ready_v, local,
 ):
     iv = lax.axis_index("val")
     ic = lax.axis_index("cond")
@@ -110,6 +110,8 @@
     core = lax.rem(iv, 2)
     hub = iv - core
     scout = hub + 1
+    chip = iv // 2
+    chips = nv // 2
     is_hub = core == 0
     is_scout = core == 1
 
@@ -137,14 +139,19 @@
     def _():
         signal(barrier, hub, ic)
 
-    each(1, nv // 2, lambda k: signal(barrier, lax.rem(hub + 2 * k, nv), ic))
-
-    wave_copy = pltpu.make_async_copy(wave, own_wave, local.at[0])
+    each(chip + 1, chips, lambda k: signal(barrier, 2 * k, ic))
+
+    @pl.when(ic == 0)
+    def _():
+        each(chip + 1, chips, lambda k: signal(barrier, 2 * k + 1, ic))
+
+
+    wave_copy = pltpu.make_async_copy(wave, own_wave, local)
     own_copies = [
-        pltpu.make_async_copy(cond, gath_c.at[ic], local.at[1]),
-        pltpu.make_async_copy(val, gath_v.at[iv], local.at[2]),
-        pltpu.make_async_copy(cond_energy, gath_ce.at[ic], local.at[3]),
-        pltpu.make_async_copy(val_energy, gath_ve.at[iv], local.at[4]),
+        pltpu.make_async_copy(cond, gath_c.at[ic], recv_c.at[mine]),
+        pltpu.make_async_copy(val, gath_v.at[iv], recv_v),
+        pltpu.make_async_copy(cond_energy, gath_ce.at[ic], recv_ce.at[mine]),
+        pltpu.make_async_copy(val_energy, gath_ve.at[iv], recv_ve),
     ]
     wave_copy.start()
     for copy in own_copies:
@@ -160,17 +167,15 @@
         remote(v, c, cond, gath_c.at[ic], recv_c.at[mine])
         remote(v, c, cond_energy, gath_ce.at[ic], recv_ce.at[mine])
 
-    def send_val():
-        def one(k):
-            peer = lax.rem(iv + k, nv)
-            remote(peer, ic, val, gath_v.at[iv], recv_v)
-            remote(peer, ic, val_energy, gath_ve.at[iv], recv_ve)
-
-        each(1, nv, one)
-
-    def send_origin(v, c, source, first, count):
+    def send_val(peer):
+        remote(peer, ic, val, gath_v.at[iv], recv_v)
+        remote(peer, ic, val_energy, gath_ve.at[iv], recv_ve)
+
+    def send_window(v, c, source):
+        remote(v, c, source, window, recv_w)
+
+    def send_origin(v, c, first, count):
         part, energies = gath_c.at[pl.ds(first, count)], gath_ce.at[pl.ds(first, count)]
-        remote(v, c, source, window, recv_w)
         remote(v, c, part, part, recv_c.at[0])
         remote(v, c, energies, energies, recv_ce.at[0])
 
@@ -184,9 +189,14 @@
         send_cond(hub, 0)
         send_cond(scout, 0)
 
+    @pl.when(is_scout & (ic == 0) & (chip > 0))
+    def _():
+        pl.semaphore_wait(barrier, 2 * chip)
+        each(0, hub, send_val)
+
     @pl.when(is_hub)
     def _():
-        pl.semaphore_wait(barrier, nv - 1 + 2 * jnp.maximum(ic - 1, 0))
+        pl.semaphore_wait(barrier, 1 + 2 * chip + 2 * jnp.maximum(ic - 1, 0))
         signal(ready.at[ic], scout, ic)
         each(2, ic, lambda j: signal(ready.at[ic], hub, j))
 
@@ -194,8 +204,10 @@
             send_cond(hub, j)
             send_cond(scout, j)
 
+        each(0, hub, lambda v: signal(ready_v, v, ic))
         each(1, ic, both)
-        send_val()
+        send_val(scout)
+        each(0, hub, send_val)
 
     wave_copy.wait()
     for block in range(own_wave.shape[0]):
@@ -206,70 +218,147 @@
             c, s = cos_p[plane:plane + 1, :], sin_p[plane:plane + 1, :]
             cos_rows[at, lanes] = (cos_x * c - sin_x * s).astype(jnp.bfloat16)
             sin_rows[at, lanes] = (sin_x * c + cos_x * s).astype(jnp.bfloat16)
-    for copy in own_copies:
-        copy.wait()
+
+    def serve(j):
+        pl.semaphore_wait(ready.at[j], 1)
+        send_cond(hub, j)
+        send_cond(scout, j)
+
+    @pl.when(is_hub & (ic > 1) & (lax.rem(ic, 2) == 0))
+    def _():
+        serve(ic + 1)
 
     @pl.when(is_scout)
     def _():
         pl.semaphore_wait(ready.at[ic], 1)
-        send_val()
-
-    def wait_origin(first, count):
-        wait_for(gath_c.at[pl.ds(first, count)], recv_c.at[0])
-        wait_for(gath_ce.at[pl.ds(first, count)], recv_ce.at[0])
+        send_val(hub)
+
+        @pl.when(ic > 0)
+        def _():
+            each(0, hub, send_val)
+
+
+    @pl.when(chip < chips - 1)
+    def _():
+        pl.semaphore_wait(ready_v, chips - 1 - chip)
+        each(scout + 1, nv, send_val)
+
+    def wait_origin():
+        wait_for(gath_c.at[pl.ds(0, 2)], recv_c.at[0])
+        wait_for(gath_ce.at[pl.ds(0, 2)], recv_ce.at[0])
 
     own_window = own_wave.at[pl.ds(0, 1)]
 
     @pl.when(is_scout & (ic == 0))
     def _():
         pl.semaphore_wait(ready.at[1], 1)
-        send_origin(scout, 1, own_window, 0, 1)
-        wait_origin(1, 1)
-
-        def serve(j):
+        send_window(scout, 1, own_window)
+        send_cond(scout, 1)
+        wait_origin()
+
+        def serve_window(j):
             pl.semaphore_wait(ready.at[j], 1)
-            send_origin(scout, j, own_window, 0, 2)
-
-        each(2, nc, serve)
+            send_window(scout, j, own_window)
+
+            @pl.when(j > 3)
+            def _():
+                send_origin(scout, j - 2, 0, 2)
+
+        each(2, nc, serve_window)
+        each(nc - 2, nc, lambda j: send_origin(scout, j, 0, 2))
 
     @pl.when(is_hub & (ic > 1))
     def _():
-        def serve(j):
-            pl.semaphore_wait(ready.at[j], 1)
-            send_cond(hub, j)
-            send_cond(scout, j)
-
-        each(ic + 1, nc, serve)
+        each(ic + 2 - lax.rem(ic, 2), nc, serve)
+
+    @pl.when(is_scout & (ic > 0))
+    def _():
+        wait_for(window, recv_w)
+        send_window(hub, ic, window)
+
+    wait_for(gath_v, recv_v)
+    wait_for(gath_ve, recv_ve)
+
+    count = 2 * cb
+    height = nv * vb * count
+    pair = iota((1, height), 1)
+    pair_v = jnp.floor((pair + 0.5) * (1.0 / count))
+    pair_c = pair - pair_v * count
+
+    def spread(row, length, index, offset):
+        square = jnp.broadcast_to(row.astype(jnp.float32), (length, length))
+        eye = iota((length, length), 0) == iota((length, length), 1)
+        column = jnp.sum(jnp.where(eye, square, 0.0), axis=1, keepdims=True)
+        chosen = iota((length, height), 0) + offset == index
+        return jnp.sum(jnp.where(chosen, column, 0.0), axis=0, keepdims=True)
+
+    own_val = sum(spread(gath_ve[b], vb, pair_v, b * vb) for b in range(nv))
+
+    def fill(step):
+        slot = step % slots
+        if step == 0:
+            other = mine
+
+            @pl.when(mine > 0)
+            def _():
+                wait_for(gath_c.at[pl.ds(mine * 2, 2)], recv_c.at[mine])
+                wait_for(gath_ce.at[pl.ds(mine * 2, 2)], recv_ce.at[mine])
+        else:
+            other = nearest(mine, step, steps)
+            if step == 1:
+                other = jnp.where(mine > 0, 0, other)
+
+                @pl.when(is_hub & (mine > 0))
+                def _():
+                    wait_origin()
+
+            else:
+                other = jnp.where(mine > 0, nearest(mine - 1, step - 1, steps - 1) + 1, other)
+
+            @pl.when(other > 0)
+            def _():
+                wait_for(gath_c.at[pl.ds(other * 2, 2)], recv_c.at[other])
+                wait_for(gath_ce.at[pl.ds(other * 2, 2)], recv_ce.at[other])
+        at = [other * 2, other * 2 + 1]
+        orbitals = jnp.concatenate([gath_c[j] for j in at], axis=0)
+        own_cond = sum(spread(gath_ce[j], cb, pair_c, n * cb) for n, j in enumerate(at))
+        weights[0:1, slot * height:(slot + 1) * height] = 1.0 / (own_cond - own_val)
+
+        def one_block(b, carry):
+            block = gath_v[b]
+            for v in range(vb):
+                first = pl.multiple_of(slot * height + (b * vb + v) * count, count)
+                dens[pl.ds(first, count), :] = orbitals * block[v:v + 1, :]
+            return carry
+
+        lax.fori_loop(0, nv, one_block, 0, unroll=nv <= 4)
+
+    def use(step, span):
+        slot = step % slots
+        at = pl.ds(slot * height, span * height)
+        weighted = dot_t(window_table[...], dens[at, :]) * weights[0:1, slot * height:(slot + span) * height]
+        update = dot(split(weighted), dens[at, :])
+        update = update[0:2 * rows] + update[2 * rows:4 * rows]
+        totals[...] = update if step == 0 else totals[...] + update
+
+    @pl.when(mine > 0)
+    def _():
+        fill(0)
+
+    @pl.when(is_scout & (mine > 0))
+    def _():
+        wait_origin()
+        send_origin(hub, ic, 0, 2)
 
     @pl.when(ic == 0)
     def _():
-        copy = pltpu.make_async_copy(own_window, window, local.at[0])
+        copy = pltpu.make_async_copy(own_window, window, local)
         copy.start()
         copy.wait()
 
-    @pl.when(is_hub & (ic == 0))
-    def _():
-        wait_origin(1, 1)
-
-    @pl.when(ic > 0)
+    @pl.when(is_hub & (ic > 0))
     def _():
         wait_for(window, recv_w)
-
-    @pl.when(ic == 1)
-    def _():
-        wait_origin(0, 1)
-
-    @pl.when(ic > 1)
-    def _():
-        wait_origin(0, 2)
-
-    @pl.when(is_scout & (ic == 1))
-    def _():
-        send_origin(hub, ic, window, 0, 1)
-
-    @pl.when(is_scout & (ic > 1))
-    def _():
-        send_origin(hub, ic, window, 0, 2)
 
     spread_wave = jnp.broadcast_to(window[...], (8, LANES))
     first = pltpu.roll(spread_wave, lax.rem(NW - iv * rows, NW), 1)
@@ -282,73 +371,72 @@
         along_x, along_y, along_z = point_parts(iota((1, LANES), 1) + block * LANES)
         turns = modulo(wave_x * along_x + wave_y * along_y + wave_z * along_z + shift, NG)
         window_table[:, pl.ds(block * LANES, LANES)] = cos_turns(turns).astype(jnp.bfloat16)
-
-    wait_for(gath_v.at[pl.ds(0, nv - 1)], recv_v)
-    wait_for(gath_ve.at[pl.ds(0, nv - 1)], recv_ve)
-
-    count = 2 * cb
-    height = nv * vb * count
-    pair = iota((1, height), 1)
-    pair_v = jnp.floor((pair + 0.5) * (1.0 / count))
-    pair_c = pair - pair_v * count
-
-    def spread(row, length, index, offset):
-        square = jnp.broadcast_to(row.astype(jnp.float32), (length, length))
-        eye = iota((length, length), 0) == iota((length, length), 1)
-        column = jnp.sum(jnp.where(eye, square, 0.0), axis=1, keepdims=True)
-        chosen = iota((length, height), 0) + offset == index
-        return jnp.sum(jnp.where(chosen, column, 0.0), axis=0, keepdims=True)
-
-    own_val = sum(spread(gath_ve[b], vb, pair_v, b * vb) for b in range(nv))
-
-    def fill(step):
-        slot = step % slots
-        if step == 0:
-            other = mine
-            peer = flip(ic, nc)
-
-            @pl.when(mine > 0)
-            def _():
-                wait_for(gath_c.at[peer], recv_c.at[mine])
-                wait_for(gath_ce.at[peer], recv_ce.at[mine])
-        else:
-            other = nearest(mine, step, steps)
-            if step == 1:
-                other = jnp.where(mine > 0, 0, other)
-            else:
-                other = jnp.where(mine > 0, nearest(mine - 1, step - 1, steps - 1) + 1, other)
-
-            @pl.when(other > 0)
-            def _():
-                wait_for(gath_c.at[pl.ds(other * 2, 2)], recv_c.at[other])
-                wait_for(gath_ce.at[pl.ds(other * 2, 2)], recv_ce.at[other])
-        at = [other * 2, other * 2 + 1]
-        orbitals = jnp.concatenate([gath_c[j] for j in at], axis=0)
-        own_cond = sum(spread(gath_ce[j], cb, pair_c, n * cb) for n, j in enumerate(at))
-        weights[0:1, slot * height:(slot + 1) * height] = 1.0 / (own_cond - own_val)
-
-        def one_block(b, carry):
-            block = gath_v[b]
-            for v in range(vb):
-                first = pl.multiple_of(slot * height + (b * vb + v) * count, count)
-                dens[pl.ds(first, count), :] = orbitals * block[v:v + 1, :]
-            return carry
-
-        lax.fori_loop(0, nv, one_block, 0, unroll=nv <= 4)
-
-    def use(step, span):
-        slot = step % slots
-        at = pl.ds(slot * height, span * height)
-        weighted = dot_t(window_table[...], dens[at, :]) * weights[0:1, slot * height:(slot + span) * height]
-        update = dot(split(weighted), dens[at, :])
-        update = update[0:2 * rows] + update[2 * rows:4 * rows]
-        totals[...] = update if step == 0 else totals[...] + update
-
-    for step in range(0, steps, 2):
-        span = min(2, steps - step)
-        for n in range(span):
-            fill(step + n)
-        use(step, span)
+    @pl.when(is_hub & (ic == 0))
+    def _():
+        wait_origin()
+
+    @pl.when(ic == 1)
+    def _():
+        wait_origin()
+
+    @pl.when(is_scout & (ic == 1))
+    def _():
+        send_origin(hub, ic, 0, 1)
+
+
+    @pl.when(mine == 0)
+    def _():
+        fill(0)
+
+    def wait_sent():
+        def sent(conds, windows):
+            def one(j):
+                wait_for(gath_c.at[0], send)
+                wait_for(gath_ce.at[0], send)
+
+            each(0, conds, one)
+            each(0, windows, lambda j: wait_for(window, send))
+
+        wait_for(gath_v.at[pl.ds(0, nv - 1)], send)
+        wait_for(gath_ve.at[pl.ds(0, nv - 1)], send)
+
+        @pl.when(is_hub & (ic > 1))
+        def _():
+            sent(2 * (nc - 2), 0)
+
+        @pl.when(is_scout & (ic == 0))
+        def _():
+            sent(1 + 2 * (nc - 2), nc - 1)
+
+        @pl.when(is_scout & (ic == 1))
+        def _():
+            sent(3, 1)
+
+        @pl.when(is_scout & (ic > 1))
+        def _():
+            sent(4, 1)
+
+    def stages(span):
+        for step in range(0, steps, span):
+            last = min(step + span, steps)
+            if last == steps:
+                wait_sent()
+            order = list(range(max(step, 1), last))
+            if span > 2 and step == 0 and last > 2:
+                order[0:2] = [2, 1]
+            for n in order:
+                fill(n)
+            use(step, last - step)
+
+    late = is_hub & (mine > 0)
+
+    @pl.when(late)
+    def _():
+        stages(4)
+
+    @pl.when(jnp.logical_not(late))
+    def _():
+        stages(2)
 
     sums = split(totals[...])
     by_cos = dot(sums, cos_rows[...])
@@ -357,33 +445,6 @@
     by_sin = by_sin[0:2 * rows] + by_sin[2 * rows:4 * rows]
     out[0:rows, :] = by_cos[0:rows] + by_sin[rows:2 * rows]
     out[rows:2 * rows, :] = by_sin[0:rows] - by_cos[rows:2 * rows]
-
-    def sent(conds, windows):
-        def one(j):
-            wait_for(gath_c.at[0], send)
-            wait_for(gath_ce.at[0], send)
-
-        each(0, conds, one)
-        each(0, windows, lambda j: wait_for(window, send))
-
-    wait_for(gath_v.at[pl.ds(0, nv - 1)], send)
-    wait_for(gath_ve.at[pl.ds(0, nv - 1)], send)
-
-    @pl.when(is_hub & (ic > 1))
-    def _():
-        sent(2 * (nc - 2), 0)
-
-    @pl.when(is_scout & (ic == 0))
-    def _():
-        sent(1 + 2 * (nc - 2), nc - 1)
-
-    @pl.when(is_scout & (ic == 1))
-    def _():
-        sent(3, 1)
-
-    @pl.when(is_scout & (ic > 1))
-    def _():
-        sent(4, 1)
 
 
 def per_device(val_orbitals, cond_orbitals, val_energy, cond_energy, wave_index):
@@ -416,7 +477,7 @@
             pltpu.VMEM((slots * height, points), bf16),
             pltpu.VMEM((8, slots * height), f32),
             pltpu.VMEM((2 * rows, points), f32),
-            dma, dma, dma((steps,)), dma((steps,)), dma, dma, regular((nc,)), dma((5,)),
+            dma, dma, dma((steps,)), dma((steps,)), dma, dma, regular((nc,)), regular, dma,
         ],
         compiler_params=pltpu.CompilerParams(
             collective_id=0, has_side_effects=True, vmem_limit_bytes=VMEM_LIMIT

time: 11.1 us -> 10.3 us (0.928)
  the two profiles are of different devices: /device:TPU:30 before, /device:TPU:31 now
where the time goes in v3:
time: 10.3 us; the launch traced here: 10.1 us
  Pallas kernels  8.82 us (86%)
  other arithmetic  0.66 us (6%)
  between operations  0.64 us (6%)
    pallas_call x1, Pallas kernels, per_device(): pl.pallas_call(functools.partial(kernel, nv, nc, slots), out_shape=jax.Sh...  8.82 us
    mul x1, other arithmetic, per_device(): return (factor * out[0:rows], factor * out[rows:2 * rows])  0.66 us

profile of v3, /device:TPU:31, one launch (start us, length us, event | category | flops | bytes accessed | tf_op | source)
XLA Modules:
  0.0 10.1 jit_solution(779004578066094366)
XLA Ops:
  0.6 8.8 %shard_map.68 = f32[64,512]{1,0:T(8,128)S(1)} custom-call(bf16[4,768]{1,0:T(4,128)(2,1)} %val.1, bf16[8,768]{1,0:T(8,128)(2,1)} %cond.1, bf16[1,4]{1,0:T(2,128)(2,1)} %bitcast.4, bf16[1,8]{1,0:T(2,128)(2,1)} %bitcast.5, s32[4,128]{1,0:T(4,128)} %bitcast.3), custom_call_target="tpu_custom_call" | custom-call | tf_op jit(solution)/shard_map/pallas_call | solution.py:462
  9.5 0.7 %slice_multiply_fusion = (f32[32,512]{1,0:T(8,128)}, f32[32,512]{1,0:T(8,128)}) fusion(f32[64,512]{1,0:T(8,128)S(1)} %shard_map.68), kind=kLoop, calls=%fused_computation | loop fusion | flops 32768 | bytes 262144 | tf_op jit(solution)/shard_map/mul | solution.py:493

commit v4 on v3

--- a/solution.py
+++ b/solution.py
@@ -127,7 +127,7 @@
     def signal(semaphore, v, c):
         pl.semaphore_signal(semaphore, inc=1, device_id={"val": v, "cond": c}, device_id_type=MESH)
 
-    @pl.when(ic == 0)
+    @pl.when((ic == 0) & (is_scout | (chip == 0)))
     def _():
         each(1, nc, lambda j: signal(barrier, scout, nc - j))
 
@@ -184,9 +184,13 @@
 
     @pl.when(is_scout & (ic > 0))
     def _():
-        pl.semaphore_wait(barrier, 2)
+        pl.semaphore_wait(barrier, 2 - jnp.minimum(chip, 1))
         signal(ready.at[ic], scout, 0)
-        send_cond(hub, 0)
+
+        @pl.when(chip == 0)
+        def _():
+            send_cond(hub, 0)
+
         send_cond(scout, 0)
 
     @pl.when(is_scout & (ic == 0) & (chip > 0))
@@ -219,6 +223,28 @@
             cos_rows[at, lanes] = (cos_x * c - sin_x * s).astype(jnp.bfloat16)
             sin_rows[at, lanes] = (sin_x * c + cos_x * s).astype(jnp.bfloat16)
 
+    own_window = own_wave.at[pl.ds(0, 1)]
+
+    def make_window_table():
+        spread_wave = jnp.broadcast_to(window[...], (8, LANES))
+        first = pltpu.roll(spread_wave, lax.rem(NW - iv * rows, NW), 1)
+        lane = lax.broadcasted_iota(jnp.int32, (8, LANES), 1)
+        index = jnp.where(lane < rows, first, pltpu.roll(first, rows, 1))[0:1, :].astype(jnp.float32)
+        index = jnp.transpose(jnp.broadcast_to(index, (LANES, LANES)))[0:2 * rows]
+        wave_x, wave_y, wave_z = wave_parts(index)
+        shift = jnp.where(iota((2 * rows, LANES), 0) < rows, 0.0, 3 * NG / 4)
+        for block in range(points // LANES):
+            along_x, along_y, along_z = point_parts(iota((1, LANES), 1) + block * LANES)
+            turns = modulo(wave_x * along_x + wave_y * along_y + wave_z * along_z + shift, NG)
+            window_table[:, pl.ds(block * LANES, LANES)] = cos_turns(turns).astype(jnp.bfloat16)
+
+    @pl.when(ic == 0)
+    def _():
+        copy = pltpu.make_async_copy(own_window, window, local)
+        copy.start()
+        copy.wait()
+        make_window_table()
+
     def serve(j):
         pl.semaphore_wait(ready.at[j], 1)
         send_cond(hub, j)
@@ -247,8 +273,6 @@
         wait_for(gath_c.at[pl.ds(0, 2)], recv_c.at[0])
         wait_for(gath_ce.at[pl.ds(0, 2)], recv_ce.at[0])
 
-    own_window = own_wave.at[pl.ds(0, 1)]
-
     @pl.when(is_scout & (ic == 0))
     def _():
         pl.semaphore_wait(ready.at[1], 1)
@@ -256,16 +280,21 @@
         send_cond(scout, 1)
         wait_origin()
 
+        @pl.when(chip > 0)
+        def _():
+            send_origin(hub, 0, 1, 1)
+
         def serve_window(j):
             pl.semaphore_wait(ready.at[j], 1)
             send_window(scout, j, own_window)
 
-            @pl.when(j > 3)
-            def _():
-                send_origin(scout, j - 2, 0, 2)
-
-        each(2, nc, serve_window)
-        each(nc - 2, nc, lambda j: send_origin(scout, j, 0, 2))
+        def serve_pair(k):
+            serve_window(2 * k)
+            serve_window(2 * k + 1)
+            send_origin(scout, 2 * k, 0, 2)
+            send_origin(scout, 2 * k + 1, 0, 2)
+
+        each(1, steps, serve_pair)
 
     @pl.when(is_hub & (ic > 1))
     def _():
@@ -275,6 +304,7 @@
     def _():
         wait_for(window, recv_w)
         send_window(hub, ic, window)
+        make_window_table()
 
     wait_for(gath_v, recv_v)
     wait_for(gath_ve, recv_ve)
@@ -319,6 +349,13 @@
             def _():
                 wait_for(gath_c.at[pl.ds(other * 2, 2)], recv_c.at[other])
                 wait_for(gath_ce.at[pl.ds(other * 2, 2)], recv_ce.at[other])
+
+            @pl.when(is_scout & (ic == 0) & (chip > 0))
+            def _():
+                part, energies = gath_c.at[pl.ds(other * 2, 2)], gath_ce.at[pl.ds(other * 2, 2)]
+                remote(hub, ic, part, part, recv_c.at[other])
+                remote(hub, ic, energies, energies, recv_ce.at[other])
+
         at = [other * 2, other * 2 + 1]
         orbitals = jnp.concatenate([gath_c[j] for j in at], axis=0)
         own_cond = sum(spread(gath_ce[j], cb, pair_c, n * cb) for n, j in enumerate(at))
@@ -339,7 +376,17 @@
         weighted = dot_t(window_table[...], dens[at, :]) * weights[0:1, slot * height:(slot + span) * height]
         update = dot(split(weighted), dens[at, :])
         update = update[0:2 * rows] + update[2 * rows:4 * rows]
-        totals[...] = update if step == 0 else totals[...] + update
+        update = update if step == 0 else totals[...] + update
+        if step + span < steps:
+            totals[...] = update
+            return
+        sums = split(update)
+        by_cos = dot(sums, cos_rows[...])
+        by_sin = dot(sums, sin_rows[...])
+        by_cos = by_cos[0:2 * rows] + by_cos[2 * rows:4 * rows]
+        by_sin = by_sin[0:2 * rows] + by_sin[2 * rows:4 * rows]
+        out[0:rows, :] = by_cos[0:rows] + by_sin[rows:2 * rows]
+        out[rows:2 * rows, :] = by_sin[0:rows] - by_cos[rows:2 * rows]
 
     @pl.when(mine > 0)
     def _():
@@ -350,27 +397,11 @@
         wait_origin()
         send_origin(hub, ic, 0, 2)
 
-    @pl.when(ic == 0)
-    def _():
-        copy = pltpu.make_async_copy(own_window, window, local)
-        copy.start()
-        copy.wait()
-
     @pl.when(is_hub & (ic > 0))
     def _():
         wait_for(window, recv_w)
-
-    spread_wave = jnp.broadcast_to(window[...], (8, LANES))
-    first = pltpu.roll(spread_wave, lax.rem(NW - iv * rows, NW), 1)
-    lane = lax.broadcasted_iota(jnp.int32, (8, LANES), 1)
-    index = jnp.where(lane < rows, first, pltpu.roll(first, rows, 1))[0:1, :].astype(jnp.float32)
-    index = jnp.transpose(jnp.broadcast_to(index, (LANES, LANES)))[0:2 * rows]
-    wave_x, wave_y, wave_z = wave_parts(index)
-    shift = jnp.where(iota((2 * rows, LANES), 0) < rows, 0.0, 3 * NG / 4)
-    for block in range(points // LANES):
-        along_x, along_y, along_z = point_parts(iota((1, LANES), 1) + block * LANES)
-        turns = modulo(wave_x * along_x + wave_y * along_y + wave_z * along_z + shift, NG)
-        window_table[:, pl.ds(block * LANES, LANES)] = cos_turns(turns).astype(jnp.bfloat16)
+        make_window_table()
+
     @pl.when(is_hub & (ic == 0))
     def _():
         wait_origin()
@@ -388,15 +419,15 @@
     def _():
         fill(0)
 
+    def sent(conds, windows):
+        def one(j):
+            wait_for(gath_c.at[0], send)
+            wait_for(gath_ce.at[0], send)
+
+        each(0, conds, one)
+        each(0, windows, lambda j: wait_for(window, send))
+
     def wait_sent():
-        def sent(conds, windows):
-            def one(j):
-                wait_for(gath_c.at[0], send)
-                wait_for(gath_ce.at[0], send)
-
-            each(0, conds, one)
-            each(0, windows, lambda j: wait_for(window, send))
-
         wait_for(gath_v.at[pl.ds(0, nv - 1)], send)
         wait_for(gath_ve.at[pl.ds(0, nv - 1)], send)
 
@@ -404,47 +435,42 @@
         def _():
             sent(2 * (nc - 2), 0)
 
-        @pl.when(is_scout & (ic == 0))
-        def _():
-            sent(1 + 2 * (nc - 2), nc - 1)
-
         @pl.when(is_scout & (ic == 1))
         def _():
-            sent(3, 1)
+            sent(3 - jnp.minimum(chip, 1), 1)
 
         @pl.when(is_scout & (ic > 1))
         def _():
-            sent(4, 1)
-
-    def stages(span):
-        for step in range(0, steps, span):
-            last = min(step + span, steps)
-            if last == steps:
+            sent(4 - jnp.minimum(chip, 1), 1)
+
+    def stages(ends):
+        ends = [end for end in ends if end < steps] + list(range(slots, steps + 1, slots))
+        step = 0
+        for end in sorted(set(ends + [steps])):
+            if end == steps:
                 wait_sent()
-            order = list(range(max(step, 1), last))
-            if span > 2 and step == 0 and last > 2:
+            order = list(range(max(step, 1), end))
+            if step == 0 and end > 2:
                 order[0:2] = [2, 1]
             for n in order:
                 fill(n)
-            use(step, last - step)
+            use(step, end - step)
+            step = end
 
     late = is_hub & (mine > 0)
 
     @pl.when(late)
     def _():
-        stages(4)
+        stages([3])
 
     @pl.when(jnp.logical_not(late))
     def _():
-        stages(2)
-
-    sums = split(totals[...])
-    by_cos = dot(sums, cos_rows[...])
-    by_sin = dot(sums, sin_rows[...])
-    by_cos = by_cos[0:2 * rows] + by_cos[2 * rows:4 * rows]
-    by_sin = by_sin[0:2 * rows] + by_sin[2 * rows:4 * rows]
-    out[0:rows, :] = by_cos[0:rows] + by_sin[rows:2 * rows]
-    out[rows:2 * rows, :] = by_sin[0:rows] - by_cos[rows:2 * rows]
+        stages([2])
+
+
+    @pl.when(is_scout & (ic == 0))
+    def _():
+        sent(1 + 2 * (nc - 2) + (nc - 1) * jnp.minimum(chip, 1), nc - 1)
 
 
 def per_device(val_orbitals, cond_orbitals, val_energy, cond_energy, wave_index):

time: 10.3 us -> 9.99 us (0.970)
  the two profiles are of different devices: /device:TPU:31 before, /device:TPU:25 now
where the time goes in v4:
time: 9.99 us; the launch traced here: 9.82 us
  Pallas kernels  8.52 us (85%)
  other arithmetic  0.66 us (7%)
  between operations  0.64 us (6%)
    pallas_call x1, Pallas kernels, per_device(): pl.pallas_call(functools.partial(kernel, nv, nc, slots), out_shape=jax.Sh...  8.52 us
    mul x1, other arithmetic, per_device(): return (factor * out[0:rows], factor * out[rows:2 * rows])  0.66 us

profile of v4, /device:TPU:25, one launch (start us, length us, event | category | flops | bytes accessed | tf_op | source)
XLA Modules:
  0.0 9.8 jit_solution(8968506091706419872)
XLA Ops:
  0.6 8.5 %shard_map.68 = f32[64,512]{1,0:T(8,128)S(1)} custom-call(bf16[4,768]{1,0:T(4,128)(2,1)} %val.1, bf16[8,768]{1,0:T(8,128)(2,1)} %cond.1, bf16[1,4]{1,0:T(2,128)(2,1)} %bitcast.4, bf16[1,8]{1,0:T(2,128)(2,1)} %bitcast.5, s32[4,128]{1,0:T(4,128)} %bitcast.3), custom_call_target="tpu_custom_call" | custom-call | tf_op jit(solution)/shard_map/pallas_call | solution.py:488
  9.2 0.7 %slice_multiply_fusion = (f32[32,512]{1,0:T(8,128)}, f32[32,512]{1,0:T(8,128)}) fusion(f32[64,512]{1,0:T(8,128)S(1)} %shard_map.68), kind=kLoop, calls=%fused_computation | loop fusion | flops 32768 | bytes 262144 | tf_op jit(solution)/shard_map/mul | solution.py:519

commit v5 on v4

--- a/solution.py
+++ b/solution.py
@@ -114,6 +114,7 @@
     chips = nv // 2
     is_hub = core == 0
     is_scout = core == 1
+    pairs = is_scout & (ic > 1) & (lax.rem(ic, 2) == 0)
 
     barrier = pltpu.get_barrier_semaphore()
 
@@ -131,7 +132,7 @@
     def _():
         each(1, nc, lambda j: signal(barrier, scout, nc - j))
 
-    @pl.when(ic > 0)
+    @pl.when(is_scout & (ic > 0))
     def _():
         each(ic + 1, nc, lambda j: signal(barrier, hub, j))
 
@@ -157,9 +158,9 @@
     for copy in own_copies:
         copy.start()
 
-    def remote(v, c, src, dst, semaphore):
+    def remote(v, c, src, dst, semaphore, late=0):
         pltpu.make_async_remote_copy(
-            src_ref=src, dst_ref=dst, send_sem=send, recv_sem=semaphore,
+            src_ref=src, dst_ref=dst, send_sem=send.at[late], recv_sem=semaphore,
             device_id={"val": v, "cond": c}, device_id_type=MESH,
         ).start()
 
@@ -200,16 +201,12 @@
 
     @pl.when(is_hub)
     def _():
-        pl.semaphore_wait(barrier, 1 + 2 * chip + 2 * jnp.maximum(ic - 1, 0))
+        pl.semaphore_wait(barrier, 1 + 2 * chip + jnp.maximum(ic - 1, 0))
         signal(ready.at[ic], scout, ic)
-        each(2, ic, lambda j: signal(ready.at[ic], hub, j))
-
-        def both(j):
-            send_cond(hub, j)
-            send_cond(scout, j)
+        each(2, ic, lambda j: signal(ready.at[ic], scout, j))
 
         each(0, hub, lambda v: signal(ready_v, v, ic))
-        each(1, ic, both)
+        each(1, ic, lambda j: send_cond(scout, j))
         send_val(scout)
         each(0, hub, send_val)
 
@@ -250,10 +247,6 @@
         send_cond(hub, j)
         send_cond(scout, j)
 
-    @pl.when(is_hub & (ic > 1) & (lax.rem(ic, 2) == 0))
-    def _():
-        serve(ic + 1)
-
     @pl.when(is_scout)
     def _():
         pl.semaphore_wait(ready.at[ic], 1)
@@ -263,15 +256,21 @@
         def _():
             each(0, hub, send_val)
 
+        @pl.when(pairs)
+        def _():
+            serve(ic + 1)
 
     @pl.when(chip < chips - 1)
     def _():
         pl.semaphore_wait(ready_v, chips - 1 - chip)
         each(scout + 1, nv, send_val)
 
+    def wait_group(g):
+        wait_for(gath_c.at[pl.ds(2 * g, 2)], recv_c.at[g])
+        wait_for(gath_ce.at[pl.ds(2 * g, 2)], recv_ce.at[g])
+
     def wait_origin():
-        wait_for(gath_c.at[pl.ds(0, 2)], recv_c.at[0])
-        wait_for(gath_ce.at[pl.ds(0, 2)], recv_ce.at[0])
+        wait_group(0)
 
     @pl.when(is_scout & (ic == 0))
     def _():
@@ -288,17 +287,36 @@
             pl.semaphore_wait(ready.at[j], 1)
             send_window(scout, j, own_window)
 
+        def send_pair(k):
+            send_origin(scout, 2 * k, 0, 2)
+            send_origin(scout, 2 * k + 1, 0, 2)
+
         def serve_pair(k):
             serve_window(2 * k)
+
+            @pl.when(k > 1)
+            def _():
+                send_pair(k - 1)
+
             serve_window(2 * k + 1)
-            send_origin(scout, 2 * k, 0, 2)
-            send_origin(scout, 2 * k + 1, 0, 2)
 
         each(1, steps, serve_pair)
-
-    @pl.when(is_hub & (ic > 1))
-    def _():
-        each(ic + 2 - lax.rem(ic, 2), nc, serve)
+        send_pair(steps - 1)
+
+    @pl.when(is_scout & (ic > 1))
+    def _():
+        def serve_both(k):
+            serve(2 * k + 1)
+            serve(2 * k)
+
+        each(mine + 1, steps, serve_both)
+
+    @pl.when(pairs)
+    def _():
+        wait_group(mine)
+        part, energies = gath_c.at[ic + 1], gath_ce.at[ic + 1]
+        remote(hub, ic, part, part, recv_c.at[mine])
+        remote(hub, ic, energies, energies, recv_ce.at[mine])
 
     @pl.when(is_scout & (ic > 0))
     def _():
@@ -329,10 +347,9 @@
         if step == 0:
             other = mine
 
-            @pl.when(mine > 0)
+            @pl.when((mine > 0) & jnp.logical_not(pairs))
             def _():
-                wait_for(gath_c.at[pl.ds(mine * 2, 2)], recv_c.at[mine])
-                wait_for(gath_ce.at[pl.ds(mine * 2, 2)], recv_ce.at[mine])
+                wait_group(mine)
         else:
             other = nearest(mine, step, steps)
             if step == 1:
@@ -347,14 +364,13 @@
 
             @pl.when(other > 0)
             def _():
-                wait_for(gath_c.at[pl.ds(other * 2, 2)], recv_c.at[other])
-                wait_for(gath_ce.at[pl.ds(other * 2, 2)], recv_ce.at[other])
-
-            @pl.when(is_scout & (ic == 0) & (chip > 0))
+                wait_group(other)
+
+            @pl.when(is_scout & (other > mine) & (ic + chip > 0))
             def _():
                 part, energies = gath_c.at[pl.ds(other * 2, 2)], gath_ce.at[pl.ds(other * 2, 2)]
-                remote(hub, ic, part, part, recv_c.at[other])
-                remote(hub, ic, energies, energies, recv_ce.at[other])
+                remote(hub, ic, part, part, recv_c.at[other], 1)
+                remote(hub, ic, energies, energies, recv_ce.at[other], 1)
 
         at = [other * 2, other * 2 + 1]
         orbitals = jnp.concatenate([gath_c[j] for j in at], axis=0)
@@ -397,6 +413,12 @@
         wait_origin()
         send_origin(hub, ic, 0, 2)
 
+    outer = mine == steps - 1
+
+    @pl.when(is_hub & outer)
+    def _():
+        fill(2)
+
     @pl.when(is_hub & (ic > 0))
     def _():
         wait_for(window, recv_w)
@@ -421,56 +443,74 @@
 
     def sent(conds, windows):
         def one(j):
-            wait_for(gath_c.at[0], send)
-            wait_for(gath_ce.at[0], send)
+            wait_for(gath_c.at[0], send.at[0])
+            wait_for(gath_ce.at[0], send.at[0])
 
         each(0, conds, one)
-        each(0, windows, lambda j: wait_for(window, send))
+        each(0, windows, lambda j: wait_for(window, send.at[0]))
 
     def wait_sent():
-        wait_for(gath_v.at[pl.ds(0, nv - 1)], send)
-        wait_for(gath_ve.at[pl.ds(0, nv - 1)], send)
-
-        @pl.when(is_hub & (ic > 1))
-        def _():
-            sent(2 * (nc - 2), 0)
+        wait_for(gath_v.at[pl.ds(0, nv - 1)], send.at[0])
+        wait_for(gath_ve.at[pl.ds(0, nv - 1)], send.at[0])
+
+        @pl.when(is_hub)
+        def _():
+            sent(jnp.maximum(ic - 1, 0), 0)
+
+        direct = 2 - jnp.minimum(chip, 1)
 
         @pl.when(is_scout & (ic == 1))
         def _():
-            sent(3 - jnp.minimum(chip, 1), 1)
+            sent(direct + 1, 1)
 
         @pl.when(is_scout & (ic > 1))
         def _():
-            sent(4 - jnp.minimum(chip, 1), 1)
-
-    def stages(ends):
+            sent(direct + 2 + 2 * (nc - 1 - ic) + 1 - lax.rem(ic, 2), 1)
+
+    def stages(ends, ahead=False, done=()):
         ends = [end for end in ends if end < steps] + list(range(slots, steps + 1, slots))
-        step = 0
+        step = filled = 0
         for end in sorted(set(ends + [steps])):
             if end == steps:
                 wait_sent()
-            order = list(range(max(step, 1), end))
-            if step == 0 and end > 2:
+            order = list(range(max(filled, 1), min(slots, steps) if ahead and end < slots else end))
+            if 1 in order and 2 in order and not ahead:
                 order[0:2] = [2, 1]
             for n in order:
-                fill(n)
+                if n not in done:
+                    fill(n)
+            filled = max([filled] + [n + 1 for n in order])
             use(step, end - step)
             step = end
 
-    late = is_hub & (mine > 0)
-
-    @pl.when(late)
+    @pl.when((is_hub & (mine > 0) & (mine < steps - 1)) | (is_scout & outer))
     def _():
         stages([3])
 
-    @pl.when(jnp.logical_not(late))
+    @pl.when(is_hub & outer)
+    def _():
+        stages([3], done={2})
+
+    @pl.when(is_scout & (mine > 0) & (mine < steps - 1))
+    def _():
+        stages([2], ahead=True)
+
+    @pl.when(mine == 0)
     def _():
         stages([2])
 
 
     @pl.when(is_scout & (ic == 0))
     def _():
-        sent(1 + 2 * (nc - 2) + (nc - 1) * jnp.minimum(chip, 1), nc - 1)
+        sent(1 + 2 * (nc - 2) + jnp.minimum(chip, 1), nc - 1)
+
+    @pl.when(is_scout & (ic + chip > 0))
+    def _():
+        def one(j):
+            wait_for(gath_c.at[pl.ds(0, 2)], send.at[1])
+            wait_for(gath_ce.at[pl.ds(0, 2)], send.at[1])
+
+        each(mine + 1, steps, one)
 
 
 def per_device(val_orbitals, cond_orbitals, val_energy, cond_energy, wave_index):
@@ -503,7 +543,7 @@
             pltpu.VMEM((slots * height, points), bf16),
             pltpu.VMEM((8, slots * height), f32),
             pltpu.VMEM((2 * rows, points), f32),
-            dma, dma, dma((steps,)), dma((steps,)), dma, dma, regular((nc,)), regular, dma,
+            dma, dma, dma((steps,)), dma((steps,)), dma, dma((2,)), regular((nc,)), regular, dma,
         ],
         compiler_params=pltpu.CompilerParams(
             collective_id=0, has_side_effects=True, vmem_limit_bytes=VMEM_LIMIT

time: 9.99 us -> 9.95 us (level)
  the two profiles are of different devices: /device:TPU:25 before, /device:TPU:0 now
where the time goes in v5:
time: 9.95 us; the launch traced here: 9.79 us
  Pallas kernels  8.49 us (85%)
  other arithmetic  0.66 us (7%)
  between operations  0.64 us (6%)
    pallas_call x1, Pallas kernels, per_device(): pl.pallas_call(functools.partial(kernel, nv, nc, slots), out_shape=jax.Sh...  8.49 us
    mul x1, other arithmetic, per_device(): return (factor * out[0:rows], factor * out[rows:2 * rows])  0.66 us

profile of v5, /device:TPU:0, one launch (start us, length us, event | category | flops | bytes accessed | tf_op | source)
XLA Modules:
  0.0 9.8 jit_solution(141589202818004549)
XLA Ops:
  0.6 8.5 %shard_map.68 = f32[64,512]{1,0:T(8,128)S(1)} custom-call(bf16[4,768]{1,0:T(4,128)(2,1)} %val.1, bf16[8,768]{1,0:T(8,128)(2,1)} %cond.1, bf16[1,4]{1,0:T(2,128)(2,1)} %bitcast.4, bf16[1,8]{1,0:T(2,128)(2,1)} %bitcast.5, s32[4,128]{1,0:T(4,128)} %bitcast.3), custom_call_target="tpu_custom_call" | custom-call | tf_op jit(solution)/shard_map/pallas_call | solution.py:528
  9.1 0.7 %slice_multiply_fusion = (f32[32,512]{1,0:T(8,128)}, f32[32,512]{1,0:T(8,128)}) fusion(f32[64,512]{1,0:T(8,128)S(1)} %shard_map.68), kind=kLoop, calls=%fused_computation | loop fusion | flops 32768 | bytes 262144 | tf_op jit(solution)/shard_map/mul | solution.py:559

commit v6 on v5

--- a/solution.py
+++ b/solution.py
@@ -21,12 +21,13 @@
 
 
 def cos_turns(turns):
-    angle = (turns - NG / 2) * (math.pi / NG)
-    square = angle * angle
-    series = 1.0
-    for order in (10, 8, 6, 4, 2):
-        series = 1.0 - square * series * (1.0 / (order * (order + 1)))
-    sine = angle * series
+    scale = math.pi / NG
+    shifted = turns - NG / 2
+    square = shifted * shifted
+    series = 0.0
+    for order in (11, 9, 7, 5, 3, 1):
+        series = series * square + (-1.0) ** (order // 2) * scale ** order / math.factorial(order)
+    sine = series * shifted
     return 2.0 * sine * sine - 1.0
 
 
@@ -85,10 +86,10 @@
     return position + 1 - 2 * lax.rem(position, 2)
 
 
-def nearest(position, step, size):
+def nearest(position, step, size, down=False):
     both = jnp.minimum(position, size - 1 - position)
     half = (step + 1) // 2
-    near = position + half if step % 2 else position - half
+    near = position + half if step % 2 != down else position - half
     side = jnp.where(position < size - 1 - position, 1, -1)
     return jnp.where(step <= 2 * both, near, position + side * (step - both))
 
@@ -225,15 +226,16 @@
     def make_window_table():
         spread_wave = jnp.broadcast_to(window[...], (8, LANES))
         first = pltpu.roll(spread_wave, lax.rem(NW - iv * rows, NW), 1)
-        lane = lax.broadcasted_iota(jnp.int32, (8, LANES), 1)
-        index = jnp.where(lane < rows, first, pltpu.roll(first, rows, 1))[0:1, :].astype(jnp.float32)
-        index = jnp.transpose(jnp.broadcast_to(index, (LANES, LANES)))[0:2 * rows]
-        wave_x, wave_y, wave_z = wave_parts(index)
-        shift = jnp.where(iota((2 * rows, LANES), 0) < rows, 0.0, 3 * NG / 4)
+        index = jnp.broadcast_to(first[0:1, :].astype(jnp.float32), (LANES, LANES))
+        wave_x, wave_y, wave_z = wave_parts(jnp.transpose(index)[0:rows])
+        quarter = NG / 4
         for block in range(points // LANES):
+            lanes = pl.ds(block * LANES, LANES)
             along_x, along_y, along_z = point_parts(iota((1, LANES), 1) + block * LANES)
-            turns = modulo(wave_x * along_x + wave_y * along_y + wave_z * along_z + shift, NG)
-            window_table[:, pl.ds(block * LANES, LANES)] = cos_turns(turns).astype(jnp.bfloat16)
+            turns = modulo(wave_x * along_x + wave_y * along_y + wave_z * along_z, NG)
+            window_table[0:rows, lanes] = cos_turns(turns).astype(jnp.bfloat16)
+            turns = jnp.where(turns < quarter, turns + 3 * quarter, turns - quarter)
+            window_table[rows:2 * rows, lanes] = cos_turns(turns).astype(jnp.bfloat16)
 
     @pl.when(ic == 0)
     def _():
@@ -352,15 +354,13 @@
                 wait_group(mine)
         else:
             other = nearest(mine, step, steps)
-            if step == 1:
-                other = jnp.where(mine > 0, 0, other)
-
+            from_scout = 0 if step == 1 else nearest(mine - 1, step - 1, steps - 1) + 1
+            from_hub = 0 if step == 2 else nearest(mine - 1, max(step - 1, 1), steps - 1, True) + 1
+            other = jnp.where(mine > 0, jnp.where(is_hub, from_hub, from_scout), other)
+            if step == 2:
                 @pl.when(is_hub & (mine > 0))
                 def _():
                     wait_origin()
-
-            else:
-                other = jnp.where(mine > 0, nearest(mine - 1, step - 1, steps - 1) + 1, other)
 
             @pl.when(other > 0)
             def _():
@@ -417,7 +417,7 @@
 
     @pl.when(is_hub & outer)
     def _():
-        fill(2)
+        fill(1)
 
     @pl.when(is_hub & (ic > 0))
     def _():
@@ -483,19 +483,23 @@
             use(step, end - step)
             step = end
 
-    @pl.when((is_hub & (mine > 0) & (mine < steps - 1)) | (is_scout & outer))
+    @pl.when(is_scout & outer)
     def _():
         stages([3])
 
     @pl.when(is_hub & outer)
     def _():
-        stages([3], done={2})
+        stages([2], done={1})
 
     @pl.when(is_scout & (mine > 0) & (mine < steps - 1))
     def _():
         stages([2], ahead=True)
 
     @pl.when(mine == 0)
+    def _():
+        stages([2, 3])
+
+    @pl.when(is_hub & (mine > 0) & (mine < steps - 1))
     def _():
         stages([2])
 

time: 9.95 us -> 9.9 us (level)
  no operation moved by 1% of the time
where the time goes in v6:
time: 9.9 us; the launch traced here: 9.73 us
  Pallas kernels  8.44 us (85%)
  other arithmetic  0.66 us (7%)
  between operations  0.64 us (6%)
    pallas_call x1, Pallas kernels, per_device(): pl.pallas_call(functools.partial(kernel, nv, nc, slots), out_shape=jax.Sh...  8.44 us
    mul x1, other arithmetic, per_device(): return (factor * out[0:rows], factor * out[rows:2 * rows])  0.66 us

profile of v6, /device:TPU:0, one launch (start us, length us, event | category | flops | bytes accessed | tf_op | source)
XLA Modules:
  0.0 9.7 jit_solution(17100290804379692121)
XLA Ops:
  0.6 8.4 %shard_map.68 = f32[64,512]{1,0:T(8,128)S(1)} custom-call(bf16[4,768]{1,0:T(4,128)(2,1)} %val.1, bf16[8,768]{1,0:T(8,128)(2,1)} %cond.1, bf16[1,4]{1,0:T(2,128)(2,1)} %bitcast.4, bf16[1,8]{1,0:T(2,128)(2,1)} %bitcast.5, s32[4,128]{1,0:T(4,128)} %bitcast.3), custom_call_target="tpu_custom_call" | custom-call | tf_op jit(solution)/shard_map/pallas_call | solution.py:532
  9.1 0.7 %slice_multiply_fusion = (f32[32,512]{1,0:T(8,128)}, f32[32,512]{1,0:T(8,128)}) fusion(f32[64,512]{1,0:T(8,128)S(1)} %shard_map.68), kind=kLoop, calls=%fused_computation | loop fusion | flops 32768 | bytes 262144 | tf_op jit(solution)/shard_map/mul | solution.py:563

commit v7 on v6

--- a/solution.py
+++ b/solution.py
@@ -98,7 +98,7 @@
     nv, nc, slots,
     val, cond, val_energy, cond_energy, wave, out,
     gath_v, gath_c, gath_ve, gath_ce, own_wave, window, cos_rows, sin_rows, window_table, dens, weights, totals,
-    recv_v, recv_ve, recv_c, recv_ce, recv_w, send, ready, ready_v, local,
+    recv_v, recv_ve, recv_c, recv_ce, recv_w, send, ready, local,
 ):
     iv = lax.axis_index("val")
     ic = lax.axis_index("cond")
@@ -133,8 +133,26 @@
     def _():
         each(1, nc, lambda j: signal(barrier, scout, nc - j))
 
+    def remote(v, c, src, dst, semaphore, sent_on=send):
+        pltpu.make_async_remote_copy(
+            src_ref=src, dst_ref=dst, send_sem=sent_on, recv_sem=semaphore,
+            device_id={"val": v, "cond": c}, device_id_type=MESH,
+        ).start()
+
+    def send_cond(v, c):
+        remote(v, c, cond, gath_c.at[ic], recv_c.at[mine])
+        remote(v, c, cond_energy, gath_ce.at[ic], recv_ce.at[mine])
+
     @pl.when(is_scout & (ic > 0))
     def _():
+        pl.semaphore_wait(barrier, 2 - jnp.minimum(chip, 1))
+
+        @pl.when(chip == 0)
+        def _():
+            send_cond(hub, 0)
+
+        signal(ready.at[ic], scout, 0)
+        send_cond(scout, 0)
         each(ic + 1, nc, lambda j: signal(barrier, hub, j))
 
     @pl.when(is_scout)
@@ -159,16 +177,6 @@
     for copy in own_copies:
         copy.start()
 
-    def remote(v, c, src, dst, semaphore, late=0):
-        pltpu.make_async_remote_copy(
-            src_ref=src, dst_ref=dst, send_sem=send.at[late], recv_sem=semaphore,
-            device_id={"val": v, "cond": c}, device_id_type=MESH,
-        ).start()
-
-    def send_cond(v, c):
-        remote(v, c, cond, gath_c.at[ic], recv_c.at[mine])
-        remote(v, c, cond_energy, gath_ce.at[ic], recv_ce.at[mine])
-
     def send_val(peer):
         remote(peer, ic, val, gath_v.at[iv], recv_v)
         remote(peer, ic, val_energy, gath_ve.at[iv], recv_ve)
@@ -184,17 +192,6 @@
     def wait_for(part, semaphore):
         pltpu.make_async_copy(part, part, semaphore).wait()
 
-    @pl.when(is_scout & (ic > 0))
-    def _():
-        pl.semaphore_wait(barrier, 2 - jnp.minimum(chip, 1))
-        signal(ready.at[ic], scout, 0)
-
-        @pl.when(chip == 0)
-        def _():
-            send_cond(hub, 0)
-
-        send_cond(scout, 0)
-
     @pl.when(is_scout & (ic == 0) & (chip > 0))
     def _():
         pl.semaphore_wait(barrier, 2 * chip)
@@ -206,7 +203,7 @@
         signal(ready.at[ic], scout, ic)
         each(2, ic, lambda j: signal(ready.at[ic], scout, j))
 
-        each(0, hub, lambda v: signal(ready_v, v, ic))
+        each(0, hub, lambda v: signal(ready.at[ic], v, ic))
         each(1, ic, lambda j: send_cond(scout, j))
         send_val(scout)
         each(0, hub, send_val)
@@ -249,23 +246,25 @@
         send_cond(hub, j)
         send_cond(scout, j)
 
+    @pl.when(pairs)
+    def _():
+        serve(ic + 1)
+
+    expected = chips - 1 - chip + core
+
+    @pl.when(expected > 0)
+    def _():
+        pl.semaphore_wait(ready.at[ic], expected)
+
     @pl.when(is_scout)
     def _():
-        pl.semaphore_wait(ready.at[ic], 1)
         send_val(hub)
 
         @pl.when(ic > 0)
         def _():
             each(0, hub, send_val)
 
-        @pl.when(pairs)
-        def _():
-            serve(ic + 1)
-
-    @pl.when(chip < chips - 1)
-    def _():
-        pl.semaphore_wait(ready_v, chips - 1 - chip)
-        each(scout + 1, nv, send_val)
+    each(scout + 1, nv, send_val)
 
     def wait_group(g):
         wait_for(gath_c.at[pl.ds(2 * g, 2)], recv_c.at[g])
@@ -369,8 +368,8 @@
             @pl.when(is_scout & (other > mine) & (ic + chip > 0))
             def _():
                 part, energies = gath_c.at[pl.ds(other * 2, 2)], gath_ce.at[pl.ds(other * 2, 2)]
-                remote(hub, ic, part, part, recv_c.at[other], 1)
-                remote(hub, ic, energies, energies, recv_ce.at[other], 1)
+                remote(hub, ic, part, part, recv_c.at[other], local)
+                remote(hub, ic, energies, energies, recv_ce.at[other], local)
 
         at = [other * 2, other * 2 + 1]
         orbitals = jnp.concatenate([gath_c[j] for j in at], axis=0)
@@ -443,15 +442,15 @@
 
     def sent(conds, windows):
         def one(j):
-            wait_for(gath_c.at[0], send.at[0])
-            wait_for(gath_ce.at[0], send.at[0])
+            wait_for(gath_c.at[0], send)
+            wait_for(gath_ce.at[0], send)
 
         each(0, conds, one)
-        each(0, windows, lambda j: wait_for(window, send.at[0]))
+        each(0, windows, lambda j: wait_for(window, send))
 
     def wait_sent():
-        wait_for(gath_v.at[pl.ds(0, nv - 1)], send.at[0])
-        wait_for(gath_ve.at[pl.ds(0, nv - 1)], send.at[0])
+        wait_for(gath_v.at[pl.ds(0, nv - 1)], send)
+        wait_for(gath_ve.at[pl.ds(0, nv - 1)], send)
 
         @pl.when(is_hub)
         def _():
@@ -511,8 +510,8 @@
     @pl.when(is_scout & (ic + chip > 0))
     def _():
         def one(j):
-            wait_for(gath_c.at[pl.ds(0, 2)], send.at[1])
-            wait_for(gath_ce.at[pl.ds(0, 2)], send.at[1])
+            wait_for(gath_c.at[pl.ds(0, 2)], local)
+            wait_for(gath_ce.at[pl.ds(0, 2)], local)
 
         each(mine + 1, steps, one)
 
@@ -547,7 +546,7 @@
             pltpu.VMEM((slots * height, points), bf16),
             pltpu.VMEM((8, slots * height), f32),
             pltpu.VMEM((2 * rows, points), f32),
-            dma, dma, dma((steps,)), dma((steps,)), dma, dma((2,)), regular((nc,)), regular, dma,
+            dma, dma, dma((steps,)), dma((steps,)), dma, dma, regular((nc,)), dma,
         ],
         compiler_params=pltpu.CompilerParams(
             collective_id=0, has_side_effects=True, vmem_limit_bytes=VMEM_LIMIT

time: 9.9 us -> 9.79 us (0.989)
  Pallas kernels: 8.44 us -> 8.33 us
    pallas_call x1, Pallas kernels: 8.44 us -> 8.33 us  [per_device(): pl.pallas_call(functools.partial(kernel, nv, nc, slots), out_shape=jax.Sh...]
where the time goes in v7:
time: 9.79 us; the launch traced here: 9.63 us
  Pallas kernels  8.33 us (85%)
  other arithmetic  0.66 us (7%)
  between operations  0.64 us (7%)
    pallas_call x1, Pallas kernels, per_device(): pl.pallas_call(functools.partial(kernel, nv, nc, slots), out_shape=jax.Sh...  8.33 us
    mul x1, other arithmetic, per_device(): return (factor * out[0:rows], factor * out[rows:2 * rows])  0.66 us

profile of v7, /device:TPU:0, one launch (start us, length us, event | category | flops | bytes accessed | tf_op | source)
XLA Modules:
  0.0 9.6 jit_solution(15882611700147079280)
XLA Ops:
  0.6 8.3 %shard_map.68 = f32[64,512]{1,0:T(8,128)S(1)} custom-call(bf16[4,768]{1,0:T(4,128)(2,1)} %val.1, bf16[8,768]{1,0:T(8,128)(2,1)} %cond.1, bf16[1,4]{1,0:T(2,128)(2,1)} %bitcast.4, bf16[1,8]{1,0:T(2,128)(2,1)} %bitcast.5, s32[4,128]{1,0:T(4,128)} %bitcast.3), custom_call_target="tpu_custom_call" | custom-call | tf_op jit(solution)/shard_map/pallas_call | solution.py:531
  9.0 0.7 %slice_multiply_fusion = (f32[32,512]{1,0:T(8,128)}, f32[32,512]{1,0:T(8,128)}) fusion(f32[64,512]{1,0:T(8,128)S(1)} %shard_map.68), kind=kLoop, calls=%fused_computation | loop fusion | flops 32768 | bytes 262144 | tf_op jit(solution)/shard_map/mul | solution.py:562

commit v8 on v7

--- a/solution.py
+++ b/solution.py
@@ -149,7 +149,8 @@
 
         @pl.when(chip == 0)
         def _():
-            send_cond(hub, 0)
+            remote(hub, 0, cond_energy, gath_ce.at[ic], recv_ce.at[mine])
+            remote(hub, 0, cond, gath_c.at[ic], recv_c.at[mine])
 
         signal(ready.at[ic], scout, 0)
         send_cond(scout, 0)
@@ -356,10 +357,10 @@
             from_scout = 0 if step == 1 else nearest(mine - 1, step - 1, steps - 1) + 1
             from_hub = 0 if step == 2 else nearest(mine - 1, max(step - 1, 1), steps - 1, True) + 1
             other = jnp.where(mine > 0, jnp.where(is_hub, from_hub, from_scout), other)
-            if step == 2:
-                @pl.when(is_hub & (mine > 0))
-                def _():
-                    wait_origin()
+
+            @pl.when(is_hub & (mine > 0) & (other == 0))
+            def _():
+                wait_origin()
 
             @pl.when(other > 0)
             def _():

time: 9.79 us -> 9.7 us (level)
  no operation moved by 1% of the time
where the time goes in v8:
time: 9.7 us; the launch traced here: 9.54 us
  Pallas kernels  8.24 us (85%)
  other arithmetic  0.66 us (7%)
  between operations  0.64 us (7%)
    pallas_call x1, Pallas kernels, per_device(): pl.pallas_call(functools.partial(kernel, nv, nc, slots), out_shape=jax.Sh...  8.24 us
    mul x1, other arithmetic, per_device(): return (factor * out[0:rows], factor * out[rows:2 * rows])  0.66 us

profile of v8, /device:TPU:0, one launch (start us, length us, event | category | flops | bytes accessed | tf_op | source)
XLA Modules:
  0.0 9.5 jit_solution(2916294207777682213)
XLA Ops:
  0.6 8.2 %shard_map.68 = f32[64,512]{1,0:T(8,128)S(1)} custom-call(bf16[4,768]{1,0:T(4,128)(2,1)} %val.1, bf16[8,768]{1,0:T(8,128)(2,1)} %cond.1, bf16[1,4]{1,0:T(2,128)(2,1)} %bitcast.4, bf16[1,8]{1,0:T(2,128)(2,1)} %bitcast.5, s32[4,128]{1,0:T(4,128)} %bitcast.3), custom_call_target="tpu_custom_call" | custom-call | tf_op jit(solution)/shard_map/pallas_call | solution.py:532
  8.9 0.7 %slice_multiply_fusion = (f32[32,512]{1,0:T(8,128)}, f32[32,512]{1,0:T(8,128)}) fusion(f32[64,512]{1,0:T(8,128)S(1)} %shard_map.68), kind=kLoop, calls=%fused_computation | loop fusion | flops 32768 | bytes 262144 | tf_op jit(solution)/shard_map/mul | solution.py:563
